TPU v7x, 128 devices: a whole 4x4x4 slice. The times are simulated.
128 devices in a mesh: section: 8 (over x_lo, y), dp: 16 (over z, x_hi, core).
Axes of the slice: x: 4 (x_hi: 2, x_lo: 2; x = x_hi * 2 + x_lo), y: 4, z: 4, core: 2. Of those that a mesh axis runs over, the one named last changes fastest.
Arguments:
- acts: bfloat16 [8, 256, 196, 1024], P('section', 'dp'), may hold values from -8 to 8, as said below
- patches: bfloat16 [256, 196, 768], P('dp', None, 'section'), may hold values from -6 to 6
- labels: int32 [256], P('dp'), may hold values from 0 to 11263
- w_first: bfloat16 [8, 1024, 256], P('section'), may hold values from -0.1875 to 0.1875
- w_second: bfloat16 [8, 256, 1024], P('section'), may hold values from -0.375 to 0.375
- w_decode: bfloat16 [8, 1024, 768], P('section'), may hold values from -0.1875 to 0.1875
- w_aux: bfloat16 [8, 1024, 512], P('section'), may hold values from -0.1875 to 0.1875
- w_class: bfloat16 [8, 11264, 512], P('section', 'dp'), may hold values from -1.5 to 1.5
Outputs:
- grad_first: float32 [8, 1024, 256], P('section', 'dp')
- grad_second: float32 [8, 256, 1024], P('section', 'dp')
- grad_decode: float32 [8, 1024, 768], P('section', 'dp')
- grad_aux: float32 [8, 1024, 512], P('section', 'dp')
- grad_class: float32 [8, 11264, 512], P('section', 'dp')
Inputs may be any that keep to these rules, and one draw needn't show every extreme that they name: `acts`: feature maps with a per-image, per-channel offset.
All inputs are finite; a program needn't handle non-finite values.
Results may differ from a plain program's by a relative error of at most 0.03.
The roundings to bfloat16 on the way count: a program that leaves them out, or rounds other values in their place, can miss the bound.
Values may be sent and summed in bfloat16 or wider, within the bound.
A program may use at most 192 MiB of HBM per device.

v0:
```python
import jax
import jax.numpy as jnp
from jax import lax
from jax.sharding import PartitionSpec as P

C = 1024
PIX = 196
PATCH = 768
CLASSES = 11264


def local(acts, patches, labels, w_first, w_second, w_decode, w_aux, w_class):
    local_acts = acts[0]
    images_here = local_acts.shape[0]
    rows_here = images_here * PIX
    flat = local_acts.reshape(rows_here, C)
    groups = lax.axis_size("dp")
    total_rows = groups * rows_here
    total_images = groups * images_here
    first = w_first[0]
    second = w_second[0]
    decode = w_decode[0]
    aux = w_aux[0]
    class_shard = w_class[0]
    target = lax.all_gather(patches, "section", axis=2, tiled=True).reshape(rows_here, PATCH)
    pre_act = jnp.dot(flat, first, preferred_element_type=jnp.float32)
    hidden = jax.nn.relu(pre_act).astype(jnp.bfloat16)
    feature = (
        flat.astype(jnp.float32) + jnp.dot(hidden, second, preferred_element_type=jnp.float32)
    ).astype(jnp.bfloat16)
    recon = jnp.dot(feature, decode, preferred_element_type=jnp.float32)
    recon_grad = ((recon - target.astype(jnp.float32)) / total_rows**0.5).astype(jnp.bfloat16)
    pooled = jnp.mean(feature.reshape(images_here, PIX, C).astype(jnp.float32), axis=1).astype(
        jnp.bfloat16
    )
    aux_pre = jnp.dot(pooled, aux, preferred_element_type=jnp.float32)
    aux_out = jax.nn.relu(aux_pre).astype(jnp.bfloat16)
    all_rows = lax.all_gather(class_shard, "dp", axis=0, tiled=True)
    logits = jnp.dot(aux_out, all_rows.T, preferred_element_type=jnp.float32)
    top = jnp.max(logits, axis=1, keepdims=True)
    expo = jnp.exp(logits - top)
    prob = expo / jnp.sum(expo, axis=1, keepdims=True)
    onehot = (labels[:, None] == jnp.arange(CLASSES, dtype=jnp.int32)[None, :]).astype(jnp.float32)
    logit_grad = ((prob - onehot) / total_images**0.5).astype(jnp.bfloat16)
    grad_class = lax.psum_scatter(
        jnp.dot(logit_grad.T, aux_out, preferred_element_type=jnp.float32).astype(jnp.bfloat16),
        "dp",
        scatter_dimension=0,
        tiled=True,
    ).astype(jnp.float32)
    back = jnp.dot(logit_grad, all_rows, preferred_element_type=jnp.float32)
    aux_grad = jnp.where(aux_pre > 0, back, 0.0).astype(jnp.bfloat16)
    pooled_grad = jnp.dot(aux_grad, aux.T, preferred_element_type=jnp.float32)
    dec_back = jnp.dot(recon_grad, decode.T, preferred_element_type=jnp.float32)
    feature_grad = (
        (dec_back.reshape(images_here, PIX, C) + pooled_grad[:, None, :] / PIX)
        .reshape(rows_here, C)
        .astype(jnp.bfloat16)
    )
    hid_back = jnp.dot(feature_grad, second.T, preferred_element_type=jnp.float32)
    hidden_grad = jnp.where(pre_act > 0, hid_back, 0.0).astype(jnp.bfloat16)
    part_first = jnp.dot(flat.T, hidden_grad, preferred_element_type=jnp.float32)
    part_second = jnp.dot(hidden.T, feature_grad, preferred_element_type=jnp.float32)
    part_decode = jnp.dot(feature.T, recon_grad, preferred_element_type=jnp.float32)
    part_aux = jnp.dot(pooled.T, aux_grad, preferred_element_type=jnp.float32)
    grad_first, grad_second, grad_decode, grad_aux = (
        lax.psum_scatter(
            part_first.astype(jnp.bfloat16), "dp", scatter_dimension=0, tiled=True
        ).astype(jnp.float32),
        lax.psum_scatter(
            part_second.astype(jnp.bfloat16), "dp", scatter_dimension=0, tiled=True
        ).astype(jnp.float32),
        lax.psum_scatter(
            part_decode.astype(jnp.bfloat16), "dp", scatter_dimension=0, tiled=True
        ).astype(jnp.float32),
        lax.psum_scatter(
            part_aux.astype(jnp.bfloat16), "dp", scatter_dimension=0, tiled=True
        ).astype(jnp.float32),
    )
    return (
        grad_first[None],
        grad_second[None],
        grad_decode[None],
        grad_aux[None],
        grad_class[None],
    )


def solution(mesh):
    in_specs = (
        P("section", "dp", None, None),
        P("dp", None, "section"),
        P("dp"),
        P("section", None, None),
        P("section", None, None),
        P("section", None, None),
        P("section", None, None),
        P("section", "dp", None),
    )
    out_specs = (
        P("section", "dp", None),
        P("section", "dp", None),
        P("section", "dp", None),
        P("section", "dp", None),
        P("section", "dp", None),
    )
    return jax.shard_map(local, mesh=mesh, in_specs=in_specs, out_specs=out_specs, check_vma=False)
```

profile of v0, /device:TPU:1, one launch (start us, length us, event | category | flops | bytes accessed | tf_op | source)
XLA Modules:
  0.0 580.6 jit_solution(17167699749627369067)
XLA Ops:
  7.2 2.6 copy.27
  10.6 9.2 %copy.26 = bf16[1,16,196,1024]{3,2,1,0:T(8,128)(2,1)} copy(bf16[1,16,196,1024]{3,1,2,0:T(8,128)(2,1)} %param.8) | data formatting | bytes 12845056 | tf_op args[0]
  19.8 8.4 %reshape_squeeze.3 = bf16[3136,1024]{1,0:T(8,128)(2,1)} reshape(bf16[1,16,196,1024]{3,2,1,0:T(8,128)(2,1)} %copy.26) | data formatting | bytes 12845056 | tf_op jit(solution)/shard_map/reshape;squeeze | solution.py:16
  28.2 4.9 fusion.21
  33.1 1.7 copy-done.3
  34.8 4.5 add_convert_fusion.1
  39.3 9.1 %reshape.27 = f32[16,196,1024]{2,1,0:T(8,128)} reshape(bf16[3136,1024]{1,0:T(8,128)(2,1)} %add_convert_fusion.1) | data formatting | bytes 19267584 | tf_op jit(solution)/shard_map/convert_element_type | solution.py:33
  48.5 6.6 %reduce_sum.18 = f32[16,1024]{1,0:T(8,128)S(1)} reduce(f32[16,196,1024]{2,1,0:T(8,128)} %reshape.27, f32[]{:T(128)} %constant.6.clone.1), dimensions={1}, to_apply=%region_0.1 | reduce | flops 3194880 | bytes 12910596 | tf_op jit(solution)/shard_map/reduce_sum | solution.py:33
  55.3 30.4 %all-gather.4.cloned.1.call-done = bf16[16,196,768]{1,0,2:T(8,128)(2,1)} async-done(((bf16[16,196,96]{1,0,2:T(8,128)(2,1)}), bf16[16,196,768]{1,0,2:T(8,128)(2,1)}) %all-gather.4.cloned.1.call-update) | async-done | bytes 4816912 | tf_op jit(solution)/shard_map/all_gather | solution.py:25
  85.7 9.5 %copy.28 = bf16[16,196,768]{2,0,1:T(8,128)(2,1)} copy(bf16[16,196,768]{1,0,2:T(8,128)(2,1)} %all-gather.4.cloned.1.call-done) | data formatting | bytes 9633792 | tf_op jit(solution)/shard_map/all_gather | solution.py:25
  95.3 8.1 %copy.29 = f32[16,196,768]{2,1,0:T(8,128)} copy(bf16[16,196,768]{2,0,1:T(8,128)(2,1)} %copy.28) | data formatting | bytes 14450688 | tf_op jit(solution)/shard_map/convert_element_type | solution.py:32
  103.3 9.9 %reshape.26 = f32[3136,768]{1,0:T(8,128)} reshape(f32[16,196,768]{2,1,0:T(8,128)} %copy.29) | data formatting | bytes 19267584 | tf_op jit(solution)/shard_map/convert_element_type | solution.py:32
  113.2 11.3 %multiply_convert_fusion = bf16[3136,768]{1,0:T(8,128)(2,1)} fusion(f32[3136,768]{1,0:T(8,128)} %reshape.26, bf16[3136,1024]{1,0:T(8,128)(2,1)} %add_convert_fusion.1, bf16[1,1024,768]{2,1,0:T(8,128)(2,1)S(1)} %copy-done), kind=kOutput, calls=%fused_computation.7 | convolution fusion | flops 4939726848 | bytes 22446080 | tf_op jit(solution)/shard_map/dot_general | solution.py:31
  124.5 7.5 %dot_general.47 = bf16[16,196,768]{2,1,0:T(8,128)(2,1)} reshape(bf16[3136,768]{1,0:T(8,128)(2,1)} %multiply_convert_fusion) | data formatting | bytes 9633792 | tf_op jit(solution)/shard_map/dot_general | solution.py:54
  132.0 10.0 %convolution_convert_fusion.1 = bf16[1024,768]{1,0:T(8,128)(2,1)} fusion(bf16[3136,1024]{1,0:T(8,128)(2,1)} %add_convert_fusion.1, bf16[3136,768]{1,0:T(8,128)(2,1)} %multiply_convert_fusion), kind=kOutput, calls=%fused_computation.11 | convolution fusion | flops 4933287936 | bytes 12812288 | tf_op jit(solution)/shard_map/dot_general | solution.py:64
  142.1 31.8 %all-gather.6.cloned.1.call-done = bf16[1,11264,512]{2,1,0:T(8,128)(2,1)} async-done(((bf16[1,704,512]{2,1,0:T(8,128)(2,1)}), bf16[1,11264,512]{2,1,0:T(8,128)(2,1)}) %all-gather.6.cloned.1.call-update) | async-done | bytes 11534352 | tf_op jit(solution)/shard_map/all_gather | solution.py:38
  173.9 7.6 %fusion.30 = (f32[16]{0:T(128)S(1)}, f32[16,11264]{1,0:T(8,128)S(1)}) fusion(bf16[1,11264,512]{2,1,0:T(8,128)(2,1)} %all-gather.6.cloned.1.call-done, f32[16,512]{1,0:T(8,128)S(1)} %fusion.15), kind=kOutput, calls=%fused_computation.46 | convolution fusion | flops 184745968 | bytes 12288064 | tf_op jit(solution)/shard_map/dot_general | solution.py:39
  181.9 1.6 fusion.11
  184.1 7.5 %add_convert_fusion = bf16[16,196,1024]{2,1,0:T(8,128)(2,1)} fusion(bf16[16,196,768]{2,1,0:T(8,128)(2,1)S(1)} %bitcast.60, f32[16,1024]{1,0:T(8,128)S(1)} %convolution_multiply_fusion, bf16[1,1024,768]{2,1,0:T(8,128)(2,1)S(1)} %copy-done), kind=kOutput, calls=%fused_computation.1 | convolution fusion | flops 4938924032 | bytes 12877824 | tf_op jit(solution)/shard_map/dot_general | solution.py:54
  191.6 8.5 %convert_element_type.86 = bf16[3136,1024]{1,0:T(8,128)(2,1)} reshape(bf16[16,196,1024]{2,1,0:T(8,128)(2,1)} %add_convert_fusion) | data formatting | bytes 12845056 | tf_op jit(solution)/shard_map/convert_element_type | solution.py:58
  200.1 12.0 %fusion.7 = bf16[1024,256]{0,1:T(8,128)(2,1)S(1)} fusion(bf16[3136,1024]{1,0:T(8,128)(2,1)} %reshape_squeeze.3, bf16[3136,1024]{1,0:T(8,128)(2,1)} %convert_element_type.86, f32[3136,256]{1,0:T(8,128)} %copy-done.3, bf16[1,256,1024]{2,1,0:T(8,128)(2,1)S(1)} %copy-done.6), kind=kOutput, calls=%fused_computation.17 | convolution fusion | flops 3291004928 | bytes 17104896 | tf_op jit(solution)/shard_map/dot_general | solution.py:62
  213.2 6.6 %convolution_convert_fusion.3 = bf16[256,1024]{1,0:T(8,128)(2,1)} fusion(bf16[3136,1024]{1,0:T(8,128)(2,1)} %convert_element_type.86, f32[3136,256]{1,0:T(8,128)} %copy-done.3), kind=kOutput, calls=%fused_computation.15 | convolution fusion | flops 1646034944 | bytes 10158080 | tf_op jit(solution)/shard_map/dot_general | solution.py:63
  219.8 1.4 convolution_convert_fusion.2
  221.3 6.2 %convolution_convert_fusion = bf16[11264,512]{1,0:T(8,128)(2,1)} fusion(f32[16,512]{1,0:T(8,128)S(1)} %fusion.15, f32[16,11264]{1,0:T(8,128)S(1)} %get-tuple-element.31, s32[16]{0:T(128)S(1)} %copy-done.7, f32[16]{0:T(128)S(1)} %fusion.17, f32[16]{0:T(128)S(1)} %get-tuple-element.30), kind=kOutput, calls=%fused_computation | convolution fusion | flops 191594496 | bytes 12288192 | tf_op jit(solution)/shard_map/dot_general | solution.py:46
  227.6 14.7 %reduce-scatter.10.cloned.1.call-done = bf16[64,768]{1,0:T(8,128)(2,1)} async-done(((bf16[1024,768]{1,0:T(8,128)(2,1)}), bf16[64,768]{1,0:T(8,128)(2,1)}) %reduce-scatter.10.cloned.1.call-update) | async-done | bytes 98320 | tf_op jit(solution)/shard_map/reduce_scatter | solution.py:73
  242.3 1.6 bitcast_convert_fusion.1
  243.9 67.0 %reduce-scatter.16.cloned.1.call-done = bf16[64,256]{1,0:T(8,128)(2,1)} async-done(((bf16[1024,256]{1,0:T(8,128)(2,1)}), bf16[64,256]{1,0:T(8,128)(2,1)}) %reduce-scatter.16.cloned.1.call-update) | async-done | bytes 32784
  312.5 66.5 %reduce-scatter.8.cloned.1.call-done = bf16[16,1024]{1,0:T(8,128)(2,1)} async-done(((bf16[256,1024]{1,0:T(8,128)(2,1)}), bf16[16,1024]{1,0:T(8,128)(2,1)}) %reduce-scatter.8.cloned.1.call-update) | async-done | bytes 32784 | tf_op jit(solution)/shard_map/reduce_scatter | solution.py:70
  380.4 69.3 %reduce-scatter.12.cloned.1.call-done = bf16[64,512]{1,0:T(8,128)(2,1)} async-done(((bf16[1024,512]{1,0:T(8,128)(2,1)}), bf16[64,512]{1,0:T(8,128)(2,1)}) %reduce-scatter.12.cloned.1.call-update) | async-done | bytes 65552 | tf_op jit(solution)/shard_map/reduce_scatter | solution.py:76
  449.8 1.5 bitcast_convert_fusion.2
  451.3 120.0 %reduce-scatter.14.cloned.1.call-done = bf16[704,512]{1,0:T(8,128)(2,1)} async-done(((bf16[11264,512]{1,0:T(8,128)(2,1)}), bf16[704,512]{1,0:T(8,128)(2,1)}) %reduce-scatter.14.cloned.1.call-update) | async-done | bytes 720912 | tf_op jit(solution)/shard_map/reduce_scatter | solution.py:45
  571.3 2.4 bitcast_convert_fusion
  (44 shorter events, 6.2 us)
Async XLA Ops:
  7.2 106.1 %copy-start = (bf16[1,1024,768]{2,1,0:T(8,128)(2,1)S(1)}, bf16[1,1024,768]{2,1,0:T(8,128)(2,1)}, u32[]{:S(2)}) copy-start(bf16[1,1024,768]{2,1,0:T(8,128)(2,1)} %param.13) | copy-start | bytes 4718596
  7.2 78.5 %all-gather.4.cloned.1.call-start = ((), (), s32[]{:S(2)}) async-start(), calls=%async_computation.5 | async-start | bytes 7077888 | tf_op jit(solution)/shard_map/all_gather | solution.py:25
  9.8 164.1 %all-gather.6.cloned.1.call-start = ((), (), s32[]{:S(2)}) async-start(), calls=%async_computation.10 | async-start | bytes 12255232 | tf_op jit(solution)/shard_map/all_gather | solution.py:38
  10.6 231.8 %reduce-scatter.10.cloned.1.call-start = ((), (), s32[]{:S(2)}) async-start(), calls=%async_computation.7 | async-start | bytes 1671168 | tf_op jit(solution)/shard_map/reduce_scatter | solution.py:73
  19.8 8.4 %copy-start.8 = (bf16[1,1024,256]{2,1,0:T(8,128)(2,1)S(1)}, bf16[1,1024,256]{2,1,0:T(8,128)(2,1)}, u32[]{:S(2)}) copy-start(bf16[1,1024,256]{2,1,0:T(8,128)(2,1)} %param.11) | copy-start | bytes 1572868
  28.2 6.5 %copy-start.2 = (bf16[3136,1024]{1,0:T(8,128)(2,1)S(1)}, bf16[3136,1024]{1,0:T(8,128)(2,1)}, u32[]{:S(2)}) copy-start(bf16[3136,1024]{1,0:T(8,128)(2,1)} %reshape_squeeze.3) | copy-start | bytes 19267588
  28.2 6.5 %copy-start.5 = (bf16[1,256,1024]{2,1,0:T(8,128)(2,1)S(1)}, bf16[1,256,1024]{2,1,0:T(8,128)(2,1)}, u32[]{:S(2)}) copy-start(bf16[1,256,1024]{2,1,0:T(8,128)(2,1)} %param.12) | copy-start | bytes 1572868
  33.1 1.7 copy-start.3
  48.5 6.6 %copy-start.4 = (bf16[1,1024,512]{2,1,0:T(8,128)(2,1)S(1)}, bf16[1,1024,512]{2,1,0:T(8,128)(2,1)}, u32[]{:S(2)}) copy-start(bf16[1,1024,512]{2,1,0:T(8,128)(2,1)} %param.14) | copy-start | bytes 3145732
  142.0 39.9 %copy-start.7 = (s32[16]{0:T(128)S(1)}, s32[16]{0:T(128)}, u32[]{:S(2)}) copy-start(s32[16]{0:T(128)} %param.10) | copy-start | bytes 196
  142.0 168.9 %reduce-scatter.16.cloned.1.call-start = ((), (), s32[]{:S(2)}) async-start(), calls=%async_computation.11 | async-start | bytes 557056
  173.9 8.0 %copy-start.1 = (bf16[1,11264,512]{2,1,0:T(8,128)(2,1)S(1)}, bf16[1,11264,512]{2,1,0:T(8,128)(2,1)}, u32[]{:S(2)}) copy-start(bf16[1,11264,512]{2,1,0:T(8,128)(2,1)} %all-gather.6.cloned.1.call-done) | copy-start | bytes 34603012
  181.5 2.4 slice-start
  181.9 2.2 slice-start.1
  191.6 8.5 %copy-start.6 = (bf16[1,256,1024]{2,1,0:T(8,128)(2,1)S(1)}, bf16[1,256,1024]{2,1,0:T(8,128)(2,1)}, u32[]{:S(2)}) copy-start(bf16[1,256,1024]{2,1,0:T(8,128)(2,1)} %param.12) | copy-start | bytes 1572868
  213.1 165.9 %reduce-scatter.8.cloned.1.call-start = ((), (), s32[]{:S(2)}) async-start(), calls=%async_computation.6 | async-start | bytes 557056 | tf_op jit(solution)/shard_map/reduce_scatter | solution.py:70
  219.8 230.0 %reduce-scatter.12.cloned.1.call-start = ((), (), s32[]{:S(2)}) async-start(), calls=%async_computation.8 | async-start | bytes 1114112 | tf_op jit(solution)/shard_map/reduce_scatter | solution.py:76
  221.3 350.0 %reduce-scatter.14.cloned.1.call-start = ((), (), s32[]{:S(2)}) async-start(), calls=%async_computation.9 | async-start | bytes 12255232 | tf_op jit(solution)/shard_map/reduce_scatter | solution.py:45
Sparse Core Ops, SparseCore 0:
  10.2 75.4 all-gather.3
  88.2 85.6 all-gather.5
  177.8 64.4 reduce-scatter.9
  246.3 64.5 reduce-scatter.15
  314.5 64.5 reduce-scatter.7
  383.7 66.0 reduce-scatter.11
  454.1 117.1 reduce-scatter.13
where the time goes:
time: 582 us; the launch traced here: 581 us
  waiting for transfers between devices  401 us (69%)
  local copies, waits for them, and re-layouts  77.2 us (13%)
  matrix products  74.3 us (13%)
  between operations  14.2 us (2%)
  other arithmetic  13.9 us (2%)
    reduce_scatter x1, waiting for transfers between devices, local(): lax.psum_scatter(jnp.dot(logit_grad.T, aux_out, preferred_element_type=jn...  120 us
    reduce_scatter x1, waiting for transfers between devices, local(): lax.psum_scatter(part_aux.astype(jnp.bfloat16), 'dp', scatter_dimension=0...  69.3 us
    unnamed x8, waiting for transfers between devices  67.8 us
    reduce_scatter x1, waiting for transfers between devices, local(): lax.psum_scatter(part_second.astype(jnp.bfloat16), 'dp', scatter_dimensio...  66.5 us
    all_gather x1, waiting for transfers between devices, local(): all_rows = lax.all_gather(class_shard, 'dp', axis=0, tiled=True)  31.8 us
    all_gather x1, waiting for transfers between devices, local(): lax.all_gather(patches, 'section', axis=2, tiled=True)  30.4 us
    convert_element_type x2, local copies, waits for them, and re-layouts, local(): target.astype(jnp.float32)  18 us
    unnamed x27, local copies, waits for them, and re-layouts  16.2 us
  transfers between devices with their start and end apart: 7, of which 7 were waited for; matrix products, arithmetic and copies ran while one was open for 27% of the time, Pallas kernels for 0%

commit v1 on v0

v1 whole, which is shorter than its diff:
```python
import functools

import jax
import jax.numpy as jnp
from jax import lax
from jax.experimental import pallas as pl
from jax.experimental.pallas import tpu as pltpu
from jax.sharding import PartitionSpec as P

MESH = pl.DeviceIdType.MESH
F32 = jnp.float32
BF16 = jnp.bfloat16

C = 1024
BOT = 256
PIX = 196
PAD = 208
PATCH = 768
HEAD = 512
CLASSES = 11264
SEC = 8
DP = 16
IMG = 16
CHUNKS = 4
PER = IMG // CHUNKS
CROWS = PER * PAD
SLICE = PATCH // SEC
PROWS = 3 * PAD
CSHARD = CLASSES // DP


def dot(a, b):
    return lax.dot_general(a, b, (((1,), (0,)), ((), ())), preferred_element_type=F32)


def dot_nt(a, b):
    return lax.dot_general(a, b, (((1,), (1,)), ((), ())), preferred_element_type=F32)


def dot_tn(a, b):
    return lax.dot_general(a, b, (((0,), (0,)), ((), ())), preferred_element_type=F32)


def permutation():
    order = []
    for tile in range(6):
        order += [SLICE * tile + lane for lane in range(96)]
        source = 6 if tile < 3 else 7
        order += [SLICE * source + 32 * (tile % 3) + lane for lane in range(32)]
    return order


def rcopy(src, dst, send, recv, dev):
    return pltpu.make_async_remote_copy(
        src_ref=src, dst_ref=dst, send_sem=send, recv_sem=recv, device_id=dev, device_id_type=MESH
    )


def kernel(
    acts, packed, labels, wf_h, ws_h, wd_h, wa_h, wc_h,
    gf, gs, gd, ga, gc,
    rawx, x, feat, hid, pat, wf, ws, wd, wa, wc,
    pooled, auxall, poolall, stats, logits, backs, backr, agall, pgrad,
    target, acc_f, acc_s, acc_d, gaacc,
    pf, ps, pd, rf, rs, rd,
    local, psend, precv, dsend, drecv,
):
    me_s = lax.axis_index("section")
    me_d = lax.axis_index("dp")

    def act_copy(image):
        return pltpu.make_async_copy(
            acts.at[0, image], rawx.at[image], local.at[image]
        )

    own_copy = pltpu.make_async_copy(packed, pat.at[me_s], local.at[16])
    own_copy.start()
    weights = [
        pltpu.make_async_copy(src.at[0], dst, local.at[17 + i])
        for i, (src, dst) in enumerate(((wf_h, wf), (ws_h, ws), (wa_h, wa), (wc_h, wc)))
    ] + [pltpu.make_async_copy(wd_h, wd, local.at[21])]
    weights[0].start()
    weights[1].start()
    for image in range(IMG):
        act_copy(image).start()
    for copy in weights[2:]:
        copy.start()

    barrier = pltpu.get_barrier_semaphore()

    def greet_s(k, _):
        pl.semaphore_signal(barrier, inc=1, device_id={"section": lax.rem(me_s + k, SEC)}, device_id_type=MESH)
        return 0

    def greet_d(k, _):
        pl.semaphore_signal(barrier, inc=1, device_id={"dp": lax.rem(me_d + k, DP)}, device_id_type=MESH)
        return 0

    lax.fori_loop(1, SEC, greet_s, 0)
    lax.fori_loop(1, DP, greet_d, 0)
    pl.semaphore_wait(barrier, SEC - 1 + DP - 1)

    own_copy.wait()

    def patch_copy(chunk, peer):
        return rcopy(
            pat.at[me_s, chunk], pat.at[me_s, chunk],
            psend.at[chunk, peer], precv.at[chunk, me_s], {"section": peer},
        )

    for chunk in range(CHUNKS):
        def send_patch(k, _, chunk=chunk):
            patch_copy(chunk, lax.rem(me_s + k, SEC)).start()
            return 0

        lax.fori_loop(1, SEC, send_patch, 0)

    weights[0].wait()
    weights[1].wait()

    def forward(chunk, _):
        base = pl.multiple_of(chunk * CROWS, CROWS)

        def wait_act(a, _):
            image = chunk * PER + a
            pltpu.make_async_copy(
                acts.at[0, image], rawx.at[image], local.at[image]
            ).wait()
            start = pl.multiple_of(image * PAD, PAD)
            x[pl.ds(start + 192, 16), :] = jnp.zeros((16, C), BF16)
            x[pl.ds(start, PIX), :] = rawx[image]
            return 0

        lax.fori_loop(0, PER, wait_act, 0)
        xc = x[pl.ds(base, CROWS), :]
        h = jnp.maximum(dot(xc, wf[...]), 0.0).astype(BF16)
        hid[pl.ds(base, CROWS), :] = h
        f = (xc.astype(F32) + dot(h, ws[...])).astype(BF16)
        feat[pl.ds(base, CROWS), :] = f
        for a in range(PER):
            part = f[a * PAD:(a + 1) * PAD, :].astype(F32)
            pooled[pl.ds(chunk * PER + a, 1), :] = jnp.sum(part, axis=0, keepdims=True) * (1.0 / PIX)
        return 0

    lax.fori_loop(0, CHUNKS, forward, 0)

    def spread(kind, src, dst):
        def one(k, _):
            peer = lax.rem(me_d + k, DP)
            rcopy(src(peer), dst, dsend.at[kind, peer], drecv.at[kind, me_d], {"dp": peer}).start()
            return 0

        lax.fori_loop(1, DP, one, 0)

    def collect(kind, slot):
        def one(k, _):
            peer = lax.rem(me_d + k, DP)
            rcopy(slot(peer), slot(peer), dsend.at[kind, peer], drecv.at[kind, peer], {"dp": peer}).wait_recv()
            return 0

        lax.fori_loop(1, DP, one, 0)

    weights[2].wait()
    weights[3].wait()
    weights[4].wait()
    pool_b = pooled[...].astype(BF16)
    aux_out = jnp.maximum(dot(pool_b, wa[...]), 0.0).astype(BF16)
    auxall[me_d] = aux_out
    spread(0, lambda peer: auxall.at[me_d], auxall.at[me_d])
    for block in range(8):
        poolall[DP, block] = pool_b[:, 128 * block:128 * (block + 1)]
    poolall_own = poolall[DP, me_d // 2]
    poolall[me_d, 0] = poolall_own
    spread(1, lambda peer: poolall.at[DP, peer // 2], poolall.at[me_d, 0])

    collect(0, lambda peer: auxall.at[peer])
    every = auxall[...].reshape(DP * IMG, HEAD)
    raw = dot_nt(wc[...], every)
    logits[...] = raw
    top = jnp.max(raw, axis=0, keepdims=True)
    total = jnp.sum(jnp.exp(raw - top), axis=0, keepdims=True)
    lane = lax.broadcasted_iota(jnp.int32, (1, DP * IMG), 1)
    row = jnp.zeros((1, DP * IMG), F32)
    for image in range(IMG):
        row = jnp.where(lane == me_d * IMG + image, labels[image].astype(F32), row)
    stats[me_d] = jnp.concatenate([top, total, row, jnp.zeros((5, DP * IMG), F32)], axis=0)
    spread(2, lambda peer: stats.at[me_d], stats.at[me_d])
    collect(2, lambda peer: stats.at[peer])
    table = stats[...]
    tops, totals, rows = table[:, 0, :], table[:, 1, :], table[:, 2, :]
    high = jnp.max(tops, axis=0, keepdims=True)
    denominator = jnp.sum(totals * jnp.exp(tops - high), axis=0, keepdims=True)
    label = jnp.sum(rows, axis=0, keepdims=True).astype(jnp.int32)
    prob = jnp.exp(logits[...] - high) / denominator
    number = lax.broadcasted_iota(jnp.int32, (CSHARD, DP * IMG), 0) + me_d * CSHARD
    lg = ((prob - (number == label).astype(F32)) * 0.0625).astype(BF16)
    gc[0] = dot(lg, every)
    backs[...] = dot_tn(lg, wc[...]).reshape(DP, IMG, HEAD)
    spread(3, lambda peer: backs.at[peer], backr.at[me_d])
    backr[me_d] = backs[me_d]
    collect(3, lambda peer: backr.at[peer])
    back = jnp.sum(backr[...], axis=0)
    aux_grad = jnp.where(aux_out > 0, back, 0.0).astype(BF16)
    agall[me_d] = aux_grad
    spread(4, lambda peer: agall.at[me_d], agall.at[me_d])
    pgrad[...] = dot_nt(aux_grad, wa[...]) * (1.0 / PIX)
    collect(1, lambda peer: poolall.at[peer, 0])
    collect(4, lambda peer: agall.at[peer])
    gaacc[...] = jnp.zeros_like(gaacc)

    def aux_part(group, _):
        part = dot_tn(poolall[group, 0], agall[group]).astype(BF16)
        gaacc[...] += part.astype(F32)
        return 0

    lax.fori_loop(0, DP, aux_part, 0)
    ga[0] = gaacc[pl.ds(pl.multiple_of(64 * lax.rem(me_d, 2), 64), 64), :]

    lane96 = lax.broadcasted_iota(jnp.int32, (PAD, 128), 1)

    def backward(chunk, _):
        base = pl.multiple_of(chunk * CROWS, CROWS)

        def wait_patch(k, _):
            peer = lax.rem(me_s + k, SEC)
            rcopy(
                pat.at[peer, chunk], pat.at[peer, chunk],
                psend.at[chunk, peer], precv.at[chunk, peer], {"section": peer},
            ).wait_recv()
            return 0

        lax.fori_loop(1, SEC, wait_patch, 0)

        for tile in range(6):
            filler, sub = (6 if tile < 3 else 7), tile % 3
            columns = pl.ds(tile * 128, 128)
            for a in range(3):
                main = pat[tile, chunk, pl.ds(a * PAD, PAD), :].astype(F32)
                extra = pat[filler, chunk, pl.ds(a * PAD, PAD), :].astype(F32)
                if sub < 3:
                    extra = pltpu.roll(extra, 96 - 32 * sub, 1)
                target[pl.ds(a * PAD, PAD), columns] = jnp.where(lane96 < 96, main, extra).astype(BF16)
            p0 = pltpu.roll(pat[tile, chunk, pl.ds(0, PAD), :].astype(F32), 32, 1)
            p1 = pltpu.roll(pat[tile, chunk, pl.ds(PAD, PAD), :].astype(F32), 64, 1)
            p2 = pltpu.roll(pat[tile, chunk, pl.ds(2 * PAD, PAD), :].astype(F32), 96, 1)
            extra = pat[filler, chunk, pl.ds(sub * PAD, PAD), :].astype(F32)
            last = jnp.where(lane96 < 32, p0, jnp.where(lane96 < 64, p1, jnp.where(lane96 < 96, p2, extra)))
            target[pl.ds(3 * PAD, PAD), columns] = last.astype(BF16)

        f = feat[pl.ds(base, CROWS), :]
        recon = dot(f, wd[...])
        rg = ((recon - target[...].astype(F32)) * (1.0 / 224.0)).astype(BF16)
        part = dot_tn(f, rg)

        @pl.when(chunk == 0)
        def _():
            acc_d[...] = part

        @pl.when(chunk > 0)
        def _():
            acc_d[...] += part

        back = dot_nt(rg, wd[...])
        parts = []
        for a in range(PER):
            parts.append(back[a * PAD:(a + 1) * PAD, :] + pgrad[pl.ds(chunk * PER + a, 1), :])
        fg = jnp.concatenate(parts, axis=0).astype(BF16)
        h = hid[pl.ds(base, CROWS), :]
        hg = jnp.where(h > 0, dot_nt(fg, ws[...]), 0.0).astype(BF16)
        part_s = dot_tn(h, fg)
        part_f = dot_tn(x[pl.ds(base, CROWS), :], hg)

        @pl.when(chunk == 0)
        def _():
            acc_s[...] = part_s
            acc_f[...] = part_f

        @pl.when(chunk > 0)
        def _():
            acc_s[...] += part_s
            acc_f[...] += part_f

        return 0

    lax.fori_loop(0, CHUNKS, backward, 0)

    pd[...] = acc_d[...].astype(BF16).reshape(DP, 64, PATCH)
    spread(5, lambda peer: pd.at[peer], rd.at[me_d])
    pf[...] = acc_f[...].astype(BF16).reshape(DP, 64, BOT)
    spread(6, lambda peer: pf.at[peer], rf.at[me_d])
    ps[...] = acc_s[...].astype(BF16).reshape(DP, 16, C)
    spread(7, lambda peer: ps.at[peer], rs.at[me_d])
    rd[me_d] = pd[me_d]
    rf[me_d] = pf[me_d]
    rs[me_d] = ps[me_d]

    def finish(kind, got, out):
        collect(kind, lambda peer: got.at[peer])
        out[0] = got[0].astype(F32)

        def one(group, _):
            out[0] += got[group].astype(F32)
            return 0

        lax.fori_loop(1, DP, one, 0)

    finish(5, rd, gd)
    finish(6, rf, gf)
    finish(7, rs, gs)

    def drain_patch(k, _):
        peer = lax.rem(me_s + k, SEC)
        for chunk in range(CHUNKS):
            patch_copy(chunk, peer).wait_send()
        return 0

    lax.fori_loop(1, SEC, drain_patch, 0)

    def drain(k, _):
        peer = lax.rem(me_d + k, DP)
        for kind, src in (
            (0, auxall.at[me_d]), (1, poolall.at[DP, 0]), (2, stats.at[me_d]), (3, backs.at[peer]),
            (4, agall.at[me_d]), (5, pd.at[peer]), (6, pf.at[peer]), (7, ps.at[peer]),
        ):
            rcopy(src, src, dsend.at[kind, peer], drecv.at[kind, peer], {"dp": peer}).wait_send()
        return 0

    lax.fori_loop(1, DP, drain, 0)


def pack(patches):
    four = jnp.pad(patches, ((0, 0), (0, PAD - PIX), (0, 0))).reshape(CHUNKS, PER, PAD, SLICE)
    main = four[:, :3]
    extra = jnp.transpose(four[:, 3].reshape(CHUNKS, PAD, 3, 32), (0, 2, 1, 3))
    return jnp.concatenate([main, extra], axis=3).reshape(CHUNKS, PROWS, 128)


def local_step(acts, patches, labels, w_first, w_second, w_decode, w_aux, w_class):
    order = permutation()
    pieces, start = [], 0
    for tile in range(6):
        source = 6 if tile < 3 else 7
        pieces.append(w_decode[0][:, SLICE * tile:SLICE * (tile + 1)])
        begin = SLICE * source + 32 * (tile % 3)
        pieces.append(w_decode[0][:, begin:begin + 32])
    decode = jnp.concatenate(pieces, axis=1)
    any_spec = pl.BlockSpec(memory_space=pl.ANY)
    vmem = pl.BlockSpec(memory_space=pltpu.VMEM)
    shapes = [
        ((IMG, PIX, C), BF16), ((IMG * PAD, C), BF16), ((IMG * PAD, C), BF16), ((IMG * PAD, BOT), BF16),
        ((SEC, CHUNKS, PROWS, 128), BF16),
        ((C, BOT), BF16), ((BOT, C), BF16), ((C, PATCH), BF16), ((C, HEAD), BF16), ((CSHARD, HEAD), BF16),
        ((IMG, C), F32), ((DP, IMG, HEAD), BF16), ((DP + 1, 8, IMG, 128), BF16), ((DP, 8, DP * IMG), F32),
        ((CSHARD, DP * IMG), F32), ((DP, IMG, HEAD), F32), ((DP, IMG, HEAD), F32), ((DP, IMG, HEAD), BF16),
        ((IMG, C), F32),
        ((CROWS, PATCH), BF16), ((C, BOT), F32), ((BOT, C), F32), ((C, PATCH), F32), ((128, HEAD), F32),
        ((DP, 64, BOT), BF16), ((DP, 16, C), BF16), ((DP, 64, PATCH), BF16),
        ((DP, 64, BOT), BF16), ((DP, 16, C), BF16), ((DP, 64, PATCH), BF16),
    ]
    gf, gs, gd, ga, gc = pl.pallas_call(
        kernel,
        name="step",
        out_shape=(
            jax.ShapeDtypeStruct((1, 64, BOT), F32), jax.ShapeDtypeStruct((1, 16, C), F32),
            jax.ShapeDtypeStruct((1, 64, PATCH), F32), jax.ShapeDtypeStruct((1, 64, HEAD), F32),
            jax.ShapeDtypeStruct((1, CSHARD, HEAD), F32),
        ),
        in_specs=[any_spec, any_spec, pl.BlockSpec(memory_space=pltpu.SMEM)] + [any_spec] * 5,
        out_specs=[vmem] * 5,
        scratch_shapes=[pltpu.VMEM(shape, kind) for shape, kind in shapes] + [
            pltpu.SemaphoreType.DMA((22,)),
            pltpu.SemaphoreType.DMA((CHUNKS, SEC)), pltpu.SemaphoreType.DMA((CHUNKS, SEC)),
            pltpu.SemaphoreType.DMA((8, DP)), pltpu.SemaphoreType.DMA((8, DP)),
        ],
        compiler_params=pltpu.CompilerParams(
            collective_id=0, has_side_effects=True, vmem_limit_bytes=63 * 2**20
        ),
        cost_estimate=pl.CostEstimate(flops=25 * 10**9, bytes_accessed=16 * 10**6, transcendentals=400000),
    )(acts, pack(patches), labels, w_first, w_second, decode, w_aux, w_class)
    back = [None] * SEC
    for tile in range(6):
        back[tile] = gd[:, :, 128 * tile:128 * tile + SLICE]
    for source in (6, 7):
        tiles = range(3) if source == 6 else range(3, 6)
        back[source] = jnp.concatenate([gd[:, :, 128 * tile + SLICE:128 * (tile + 1)] for tile in tiles], axis=2)
    return gf, gs, jnp.concatenate(back, axis=2), ga, gc


def solution(mesh):
    in_specs = (
        P("section", "dp", None, None),
        P("dp", None, "section"),
        P("dp"),
        P("section", None, None),
        P("section", None, None),
        P("section", None, None),
        P("section", None, None),
        P("section", "dp", None),
    )
    out_specs = (P("section", "dp", None),) * 5
    return jax.shard_map(local_step, mesh=mesh, in_specs=in_specs, out_specs=out_specs, check_vma=False)
```

time: 582 us -> 196 us (0.34)
  the two profiles are of different devices: /device:TPU:1 before, /device:TPU:15 now
where the time goes in v1:
time: 196 us
  Pallas kernels  169 us (86%)
  local copies, waits for them, and re-layouts  25.9 us (13%)
    pallas_call x1, Pallas kernels, local_step(): pl.pallas_call(kernel, name='step', out_shape=(jax.ShapeDtypeStruct((1, 6...  169 us
    unnamed x11, local copies, waits for them, and re-layouts  14.1 us
    concatenate x1, local copies, waits for them, and re-layouts, local_step(): decode = jnp.concatenate(pieces, axis=1)  4.72 us

profile of v1, /device:TPU:15, one launch (start us, length us, event | category | flops | bytes accessed | tf_op | source)
XLA Modules:
  0.0 195.8 jit_solution(10993130977596843902)
XLA Ops:
  0.6 1.3 pad.4
  2.0 0.0 copy-start
  2.0 0.1 pad_maximum_fusion
  2.1 1.1 copy.18
  3.2 0.2 copy-done
  3.5 0.4 fusion
  3.9 1.5 fusion.1
  5.3 4.7 %concatenate.10.wd_h = bf16[1024,768]{1,0:T(8,128)(2,1)} concatenate(bf16[1024,96]{1,0:T(8,128)(2,1)} %get-tuple-element.26, bf16[1024,32]{1,0:T(8,128)(2,1)S(1)} %get-tuple-element.20, bf16[1024,96]{1,0:T(8,128)(2,1)} %get-tuple-element.25, bf16[1024,32]{1,0:T(8,128)(2,1)S(1)} %get-tuple-element.19, bf16[1024,96]{1,0:T(8,128)(2,1)} %get-tuple-element.24, ...), dimensions={1} | concatenate | bytes 3145728 | tf_op jit(solution)/shard_map/concatenate | solution.py:346
  10.1 9.1 %copy.19.acts = bf16[1,16,196,1024]{3,2,1,0:T(8,128)(2,1)} copy(bf16[1,16,196,1024]{3,1,2,0:T(8,128)(2,1)} %param.8) | data formatting | bytes 12845056 | tf_op args[0]
  19.2 169.1 %step.1 = (f32[1,64,256]{2,1,0:T(8,128)}, f32[1,16,1024]{2,1,0:T(8,128)}, f32[1,64,768]{2,1,0:T(8,128)}, f32[1,64,512]{2,1,0:T(8,128)}, f32[1,704,512]{2,1,0:T(8,128)}) custom-call(bf16[1,16,196,1024]{3,2,1,0:T(8,128)(2,1)} %copy.19.acts, bf16[4,624,128]{2,1,0:T(8,128)(2,1)} %bitcast.11, s32[16]{0:T(128)} %labels.1, bf16[1,1024,256]{2,1,0:T(8,128)(2,1)} %wf_h.1, ...), custom_call_target="tpu_custom_call" | custom-call | flops 24999999488 | bytes 16000000 | tf_op jit(solution)/shard_map/step/pallas_call | solution.py:360
  188.3 0.0 copy-start.2
  188.3 0.0 copy-start.1
  188.4 1.0 fusion.3
  189.3 1.0 fusion.2
  190.3 0.8 concatenate.11
  191.1 1.5 copy.24
  192.6 1.5 copy.25
  194.1 0.0 copy-done.2
  194.1 0.7 copy.26
  194.7 0.0 copy-done.1
  194.7 1.1 copy.27
  (2 shorter events, 0.1 us)
Async XLA Ops:
  2.0 1.5 copy-start
  188.3 5.7 %copy-start.2 = (f32[1,64,512]{2,1,0:T(8,128)S(1)}, f32[1,64,512]{2,1,0:T(8,128)}, u32[]{:S(2)}) copy-start(f32[1,64,512]{2,1,0:T(8,128)} %get-tuple-element.47) | copy-start | bytes 393220
  188.3 6.4 %copy-start.1 = (f32[1,704,512]{2,1,0:T(8,128)S(1)}, f32[1,704,512]{2,1,0:T(8,128)}, u32[]{:S(2)}) copy-start(f32[1,704,512]{2,1,0:T(8,128)} %get-tuple-element.48) | copy-start | bytes 4325380

commit v2 on v0

v2 whole, which is shorter than its diff:
```python
import jax
import jax.numpy as jnp
from jax import lax
from jax.experimental import pallas as pl
from jax.experimental.pallas import tpu as pltpu
from jax.sharding import PartitionSpec as P

MESH = pl.DeviceIdType.MESH
F32 = jnp.float32
BF16 = jnp.bfloat16

C = 1024
BOT = 256
PIX = 196
PATCH = 768
HEAD = 512
CLASSES = 11264
SEC = 8
DP = 16
IMG = 16
ROWS = PIX * IMG
SLICE = PATCH // SEC
CSHARD = CLASSES // DP
STARTS = (0, 768, 1536, 2304)
SIZES = (768, 768, 768, 832)
CHUNKS = len(SIZES)
PROWS = ROWS * SLICE // 128
KINDS = (2, 1, 2, 1)


def dot(a, b):
    return lax.dot_general(a, b, (((1,), (0,)), ((), ())), preferred_element_type=F32)


def dot_nt(a, b):
    return lax.dot_general(a, b, (((1,), (1,)), ((), ())), preferred_element_type=F32)


def dot_tn(a, b):
    return lax.dot_general(a, b, (((0,), (0,)), ((), ())), preferred_element_type=F32)


def rcopy(src, dst, send, recv, dev):
    return pltpu.make_async_remote_copy(
        src_ref=src, dst_ref=dst, send_sem=send, recv_sem=recv, device_id=dev, device_id_type=MESH
    )


def half_rows(chunk, half):
    start, size = STARTS[chunk] * 3 // 4, SIZES[chunk] * 3 // 4
    first = size // 32 * 16
    return pl.ds(start, first) if half == 0 else pl.ds(start + first, size - first)


def kernel(
    acts, packed, labels, wf_h, ws_h, wd_h, wa_h, wc_h,
    gf, gs, gd, ga, gc,
    x, feat, hid, pat, wf, ws, wd, wp, wa, wc, recon,
    pooled, poolb, auxall, poolall, stats, logits, backs, backr, agall, pgrad,
    target, acc_f, acc_s, acc_d, gaacc,
    pf, ps, pd, qf, qs, qd, tf, ts, td, rf, rs, rd,
    local, psend, precv, dsend, drecv, csend, crecv, tsend, trecv,
):
    me_s = lax.axis_index("section")
    me_d = lax.axis_index("dp")
    side = me_s // 4
    row = lax.rem(me_s, 4)
    core = lax.rem(me_d, 2)
    chip = me_d // 2

    def at(where, step):
        return where * 4 + lax.rem(row + step, 4)

    up, down, across = at(side, 1), at(side, 3), at(1 - side, 0)

    loads = [
        pltpu.make_async_copy(src, dst, local.at[i])
        for i, (src, dst) in enumerate(
            [(packed, pat.at[me_s]), (wf_h.at[0], wf), (ws_h.at[0], ws)]
            + [
                (acts.at[pl.ds(STARTS[c], SIZES[c]), :], x.at[pl.ds(STARTS[c], SIZES[c]), :])
                for c in range(CHUNKS)
            ]
            + [(wa_h.at[0], wa), (wd_h.at[0], wd), (wc_h.at[0], wc)]
        )
    ]
    for load in loads:
        load.start()

    barrier = pltpu.get_barrier_semaphore()
    for peer in (up, down, across):
        pl.semaphore_signal(barrier, inc=1, device_id={"section": peer}, device_id_type=MESH)

    def greet(k, _):
        pl.semaphore_signal(barrier, inc=1, device_id={"dp": lax.rem(me_d + k, DP)}, device_id_type=MESH)
        return 0

    lax.fori_loop(1, DP, greet, 0)
    pl.semaphore_wait(barrier, 3 + DP - 1)

    sent = [0] * CHUNKS
    started = []

    def pass_on(chunk, source, half, peer):
        place = pat.at[source, half_rows(chunk, half), :]
        copy = rcopy(
            place, place, psend.at[chunk, sent[chunk]], precv.at[chunk, half, source], {"section": peer}
        )
        sent[chunk] += 1
        copy.start()
        started.append(copy)

    def arrive(chunk, source, half):
        place = pat.at[source, half_rows(chunk, half), :]
        rcopy(
            place, place, psend.at[chunk, 0], precv.at[chunk, half, source], {"section": up}
        ).wait_recv()

    loads[0].wait()
    for chunk in range(CHUNKS):
        for half in range(2):
            pass_on(chunk, me_s, half, across)
            pass_on(chunk, me_s, half, up if half == 0 else down)
            pass_on(chunk, me_s, half, down if half == 0 else up)

    def stage1(chunk):
        for source, half, onward in (
            (at(side, 3), 0, up), (at(side, 1), 1, down), (at(side, 3), 1, None), (at(side, 1), 0, None)
        ):
            arrive(chunk, source, half)
            if onward is not None:
                pass_on(chunk, source, half, onward)
            if KINDS[chunk] == 1:
                pass_on(chunk, source, half, across)
        if KINDS[chunk] == 2:
            for half in range(2):
                arrive(chunk, across, half)
                pass_on(chunk, across, half, up if half == 0 else down)
                pass_on(chunk, across, half, down if half == 0 else up)

    def stage2(chunk):
        if KINDS[chunk] == 1:
            for half in range(2):
                arrive(chunk, at(side, 2), half)
                pass_on(chunk, at(side, 2), half, across)
        else:
            arrive(chunk, at(1 - side, 3), 0)
            pass_on(chunk, at(1 - side, 3), 0, up)
            arrive(chunk, at(1 - side, 1), 1)
            pass_on(chunk, at(1 - side, 1), 1, down)

    def stage3(chunk):
        if KINDS[chunk] == 1:
            for step in (0, 1, 3, 2):
                for half in range(2):
                    arrive(chunk, at(1 - side, step), half)
        else:
            arrive(chunk, at(1 - side, 3), 1)
            arrive(chunk, at(1 - side, 1), 0)
            for half in range(2):
                arrive(chunk, at(side, 2), half)
                arrive(chunk, at(1 - side, 2), half)

    def rows_of(chunk):
        return pl.ds(STARTS[chunk], SIZES[chunk])

    def forward(chunk):
        loads[3 + chunk].wait()
        xc = x[rows_of(chunk), :]
        h = jnp.maximum(dot(xc, wf[...]), 0.0).astype(BF16)
        hid[rows_of(chunk), :] = h
        f = (xc.astype(F32) + dot(h, ws[...])).astype(BF16)
        feat[rows_of(chunk), :] = f
        part = jnp.sum(f.astype(F32).reshape(SIZES[chunk] // IMG, IMG, C), axis=0)
        if chunk == 0:
            pooled[...] = part
        else:
            pooled[...] += part

    def rebuild(chunk):
        recon[rows_of(chunk), :] = dot(feat[rows_of(chunk), :], wp[...])

    def spread(kind, src, dst):
        def one(k, _):
            peer = lax.rem(me_d + k, DP)
            rcopy(src(peer), dst, dsend.at[kind, peer], drecv.at[kind, me_d], {"dp": peer}).start()
            return 0

        lax.fori_loop(1, DP, one, 0)

    def collect(kind, slot):
        def one(k, _):
            peer = lax.rem(me_d + k, DP)
            rcopy(slot(peer), slot(peer), dsend.at[kind, peer], drecv.at[kind, peer], {"dp": peer}).wait_recv()
            return 0

        lax.fori_loop(1, DP, one, 0)

    loads[1].wait()
    loads[2].wait()
    forward(0)
    forward(1)
    stage1(0)
    forward(2)
    forward(3)

    loads[7].wait()
    pool_b = (pooled[...] * (1.0 / PIX)).astype(BF16)
    aux_out = jnp.maximum(dot(pool_b, wa[...]), 0.0).astype(BF16)
    auxall[me_d] = aux_out
    spread(0, lambda peer: auxall.at[me_d], auxall.at[me_d])
    for block in range(8):
        poolb[block] = pool_b[:, 128 * block:128 * (block + 1)]
    poolall[me_d] = poolb[chip]
    spread(1, lambda peer: poolb.at[peer // 2], poolall.at[me_d])
    stage1(1)

    loads[8].wait()
    source = lax.broadcasted_iota(jnp.int32, (PATCH, PATCH), 0)
    place = lax.broadcasted_iota(jnp.int32, (PATCH, PATCH), 1)
    tile, lane = place >> 7, place & 127
    late = (tile >= 3).astype(jnp.int32)
    origin = jnp.where(
        lane < SLICE, SLICE * tile + lane, 6 * SLICE + SLICE * late + 32 * (tile - 3 * late) + lane - SLICE
    )
    wp[...] = dot(wd[...], (source == origin).astype(F32).astype(BF16)).astype(BF16)
    rebuild(0)

    loads[9].wait()
    collect(0, lambda peer: auxall.at[peer])
    every = auxall[...].reshape(DP * IMG, HEAD)
    raw = dot_nt(wc[...], every)
    logits[...] = raw
    top = jnp.max(raw, axis=0, keepdims=True)
    total = jnp.sum(jnp.exp(raw - top), axis=0, keepdims=True)
    column = lax.broadcasted_iota(jnp.int32, (1, DP * IMG), 1)
    line = jnp.zeros((1, DP * IMG), F32)
    for image in range(IMG):
        line = jnp.where(column == me_d * IMG + image, labels[image].astype(F32), line)
    stats[me_d] = jnp.concatenate([top, total, line, jnp.zeros((5, DP * IMG), F32)], axis=0)
    spread(2, lambda peer: stats.at[me_d], stats.at[me_d])
    stage2(0)
    stage1(2)
    rebuild(1)

    collect(2, lambda peer: stats.at[peer])
    table = stats[...]
    high = jnp.max(table[:, 0, :], axis=0, keepdims=True)
    denominator = jnp.sum(table[:, 1, :] * jnp.exp(table[:, 0, :] - high), axis=0, keepdims=True)
    label = jnp.sum(table[:, 2, :], axis=0, keepdims=True).astype(jnp.int32)
    prob = jnp.exp(logits[...] - high) / denominator
    number = lax.broadcasted_iota(jnp.int32, (CSHARD, DP * IMG), 0) + me_d * CSHARD
    lg = ((prob - (number == label).astype(F32)) * 0.0625).astype(BF16)
    backs[...] = dot_tn(lg, wc[...]).reshape(DP, IMG, HEAD)
    spread(3, lambda peer: backs.at[peer], backr.at[me_d])
    backr[me_d] = backs[me_d]
    gc[0] = dot(lg, every)
    stage2(1)
    stage1(3)
    rebuild(2)

    collect(3, lambda peer: backr.at[peer])
    aux_grad = jnp.where(auxall[me_d] > 0, jnp.sum(backr[...], axis=0), 0.0).astype(BF16)
    agall[me_d] = aux_grad
    spread(4, lambda peer: agall.at[me_d], agall.at[me_d])
    pgrad[...] = dot_nt(aux_grad, wa[...]) * (1.0 / PIX)
    stage2(2)
    stage2(3)
    rebuild(3)

    def assemble(chunk):
        q = SIZES[chunk] // 4
        base = STARTS[chunk] * 3 // 4
        cut = lax.broadcasted_iota(jnp.int32, (q, 128), 1)
        for tile in range(6):
            filler, sub = (6 if tile < 3 else 7), tile % 3
            columns = pl.ds(tile * 128, 128)
            blocks = [pat[tile, pl.ds(base + a * q, q), :].astype(F32) for a in range(3)]
            for a in range(3):
                extra = pltpu.roll(pat[filler, pl.ds(base + a * q, q), :].astype(F32), 96 - 32 * sub, 1)
                target[pl.ds(a * q, q), columns] = jnp.where(cut < 96, blocks[a], extra).astype(BF16)
            turned = [pltpu.roll(blocks[a], 32 * (a + 1), 1) for a in range(3)]
            extra = pat[filler, pl.ds(base + sub * q, q), :].astype(F32)
            last = jnp.where(cut < 64, jnp.where(cut < 32, turned[0], turned[1]), jnp.where(cut < 96, turned[2], extra))
            target[pl.ds(3 * q, q), columns] = last.astype(BF16)

    def decode_grad(chunk):
        stage3(chunk)
        assemble(chunk)
        size = SIZES[chunk]
        rg = ((recon[rows_of(chunk), :] - target[pl.ds(0, size), :].astype(F32)) * (1.0 / 224.0)).astype(BF16)
        part = dot_tn(feat[rows_of(chunk), :], rg)
        if chunk == 0:
            acc_d[...] = part
        else:
            acc_d[...] += part
        return rg

    def feature_grad(chunk, rg):
        size = SIZES[chunk]
        back = dot_nt(rg, wp[...]).reshape(size // IMG, IMG, C) + pgrad[...][None]
        fg = back.reshape(size, C).astype(BF16)
        h = hid[rows_of(chunk), :]
        hg = jnp.where(h > 0, dot_nt(fg, ws[...]), 0.0).astype(BF16)
        return fg, hg

    def module_grads(chunk, fg, hg):
        part_s = dot_tn(hid[rows_of(chunk), :], fg)
        part_f = dot_tn(x[rows_of(chunk), :], hg)
        if chunk == 0:
            acc_s[...] = part_s
            acc_f[...] = part_f
        else:
            acc_s[...] += part_s
            acc_f[...] += part_f

    for chunk in range(CHUNKS - 1):
        rg = decode_grad(chunk)
        module_grads(chunk, *feature_grad(chunk, rg))

    collect(1, lambda peer: poolall.at[peer])
    collect(4, lambda peer: agall.at[peer])
    gaacc[...] = jnp.zeros_like(gaacc)

    def aux_part(group, _):
        gaacc[...] += dot_tn(poolall[group], agall[group]).astype(BF16).astype(F32)
        return 0

    lax.fori_loop(0, DP, aux_part, 0)
    ga[0] = gaacc[pl.ds(pl.multiple_of(64 * core, 64), 64), :]

    def pair(kind, mine, theirs):
        return rcopy(mine.at[1 - core], theirs, csend.at[kind], crecv.at[kind], {"dp": me_d + 1 - 2 * core})

    def split(acc, out, rows):
        whole = acc[...].astype(BF16).reshape(8, 2, rows, acc.shape[1])
        out[0] = whole[:, 0]
        out[1] = whole[:, 1]

    def chip_sum(kind, mine, theirs, out, got):
        pair(kind, mine, theirs).wait_recv()
        out[...] = (mine[core].astype(F32) + theirs[...].astype(F32)).astype(BF16)

        def one(k, _):
            peer = lax.rem(chip + k, 8)
            rcopy(
                out.at[peer], got.at[chip], tsend.at[kind, peer], trecv.at[kind, chip], {"dp": 2 * peer + core}
            ).start()
            return 0

        lax.fori_loop(1, 8, one, 0)
        got[chip] = out[chip]

    def total_sum(kind, got):
        def one(k, _):
            peer = lax.rem(chip + k, 8)
            rcopy(
                got.at[peer], got.at[peer], tsend.at[kind, peer], trecv.at[kind, peer], {"dp": 2 * peer + core}
            ).wait_recv()
            return 0

        lax.fori_loop(1, 8, one, 0)
        return jnp.sum(got[...].astype(F32), axis=0)

    last = CHUNKS - 1
    rg = decode_grad(last)
    split(acc_d, pd, 64)
    pair(0, pd, qd).start()
    fg, hg = feature_grad(last, rg)
    chip_sum(0, pd, qd, td, rd)
    module_grads(last, fg, hg)
    split(acc_f, pf, 64)
    pair(1, pf, qf).start()
    split(acc_s, ps, 16)
    pair(2, ps, qs).start()
    chip_sum(1, pf, qf, tf, rf)
    chip_sum(2, ps, qs, ts, rs)

    gsum = total_sum(0, rd)
    for s in range(SEC):
        if s < 6:
            gd[0, :, SLICE * s:SLICE * (s + 1)] = gsum[:, 128 * s:128 * s + SLICE]
        else:
            for sub in range(3):
                begin = 128 * (3 * (s - 6) + sub) + SLICE
                gd[0, :, SLICE * s + 32 * sub:SLICE * s + 32 * (sub + 1)] = gsum[:, begin:begin + 32]
    gf[0] = total_sum(1, rf)
    gs[0] = total_sum(2, rs)

    for copy in started:
        copy.wait_send()
    for kind, mine, theirs in ((0, pd, qd), (1, pf, qf), (2, ps, qs)):
        pair(kind, mine, theirs).wait_send()

    def drain(k, _):
        peer = lax.rem(me_d + k, DP)
        for kind, src in (
            (0, auxall.at[me_d]), (1, poolb.at[0]), (2, stats.at[me_d]), (3, backs.at[peer]), (4, agall.at[me_d])
        ):
            rcopy(src, src, dsend.at[kind, peer], drecv.at[kind, peer], {"dp": peer}).wait_send()
        return 0

    lax.fori_loop(1, DP, drain, 0)

    def drain_chip(k, _):
        peer = lax.rem(chip + k, 8)
        for kind, src in ((0, td), (1, tf), (2, ts)):
            rcopy(
                src.at[peer], src.at[peer], tsend.at[kind, peer], trecv.at[kind, peer], {"dp": 2 * peer + core}
            ).wait_send()
        return 0

    lax.fori_loop(1, 8, drain_chip, 0)


def pack(patches):
    rows = jnp.transpose(patches, (1, 0, 2)).reshape(ROWS, SLICE)
    parts = []
    for chunk in range(CHUNKS):
        q = SIZES[chunk] // 4
        four = lax.slice_in_dim(rows, STARTS[chunk], STARTS[chunk] + SIZES[chunk]).reshape(4, q, SLICE)
        extra = jnp.transpose(four[3].reshape(q, 3, 32), (1, 0, 2))
        parts.append(jnp.concatenate([four[:3], extra], axis=2).reshape(3 * q, 128))
    return jnp.concatenate(parts, axis=0)


def local_step(acts, patches, labels, w_first, w_second, w_decode, w_aux, w_class):
    any_spec = pl.BlockSpec(memory_space=pl.ANY)
    vmem = pl.BlockSpec(memory_space=pltpu.VMEM)
    big = max(SIZES)
    shapes = [
        ((ROWS, C), BF16), ((ROWS, C), BF16), ((ROWS, BOT), BF16), ((SEC, PROWS, 128), BF16),
        ((C, BOT), BF16), ((BOT, C), BF16), ((C, PATCH), BF16), ((C, PATCH), BF16), ((C, HEAD), BF16),
        ((CSHARD, HEAD), BF16), ((ROWS, PATCH), F32),
        ((IMG, C), F32), ((8, IMG, 128), BF16), ((DP, IMG, HEAD), BF16), ((DP, IMG, 128), BF16),
        ((DP, 8, DP * IMG), F32), ((CSHARD, DP * IMG), F32), ((DP, IMG, HEAD), F32), ((DP, IMG, HEAD), F32),
        ((DP, IMG, HEAD), BF16), ((IMG, C), F32),
        ((big, PATCH), BF16), ((C, BOT), F32), ((BOT, C), F32), ((C, PATCH), F32), ((128, HEAD), F32),
        ((2, 8, 64, BOT), BF16), ((2, 8, 16, C), BF16), ((2, 8, 64, PATCH), BF16),
    ] + [((8, 64, BOT), BF16), ((8, 16, C), BF16), ((8, 64, PATCH), BF16)] * 3
    return pl.pallas_call(
        kernel,
        name="step",
        out_shape=(
            jax.ShapeDtypeStruct((1, 64, BOT), F32), jax.ShapeDtypeStruct((1, 16, C), F32),
            jax.ShapeDtypeStruct((1, 64, PATCH), F32), jax.ShapeDtypeStruct((1, 64, HEAD), F32),
            jax.ShapeDtypeStruct((1, CSHARD, HEAD), F32),
        ),
        in_specs=[any_spec, any_spec, pl.BlockSpec(memory_space=pltpu.SMEM)] + [any_spec] * 5,
        out_specs=[vmem] * 5,
        scratch_shapes=[pltpu.VMEM(shape, kind) for shape, kind in shapes] + [
            pltpu.SemaphoreType.DMA((10,)),
            pltpu.SemaphoreType.DMA((CHUNKS, 14)), pltpu.SemaphoreType.DMA((CHUNKS, 2, SEC)),
            pltpu.SemaphoreType.DMA((5, DP)), pltpu.SemaphoreType.DMA((5, DP)),
            pltpu.SemaphoreType.DMA((3,)), pltpu.SemaphoreType.DMA((3,)),
            pltpu.SemaphoreType.DMA((3, 8)), pltpu.SemaphoreType.DMA((3, 8)),
        ],
        compiler_params=pltpu.CompilerParams(
            collective_id=0, has_side_effects=True, vmem_limit_bytes=63 * 2**20
        ),
        cost_estimate=pl.CostEstimate(flops=25 * 10**9, bytes_accessed=16 * 10**6, transcendentals=400000),
    )(
        jnp.transpose(acts[0], (1, 0, 2)).reshape(ROWS, C), pack(patches), labels,
        w_first, w_second, w_decode, w_aux, w_class,
    )


def solution(mesh):
    in_specs = (
        P("section", "dp", None, None),
        P("dp", None, "section"),
        P("dp"),
        P("section", None, None),
        P("section", None, None),
        P("section", None, None),
        P("section", None, None),
        P("section", "dp", None),
    )
    out_specs = (P("section", "dp", None),) * 5
    return jax.shard_map(local_step, mesh=mesh, in_specs=in_specs, out_specs=out_specs, check_vma=False)
```

time: 582 us -> 108 us (0.19)
  waiting for transfers between devices: 401 us -> 0 us
  Pallas kernels: 0 us -> 92.6 us
  matrix products: 74.3 us -> 0 us
  local copies, waits for them, and re-layouts: 77.2 us -> 13.2 us
  between operations: 14.2 us -> 0.75 us
  other arithmetic: 13.9 us -> 1.16 us
    reduce_scatter x4 -> x0, waiting for transfers between devices: 271 us -> none  [the longest x1 120 us: local(): lax.psum_scatter(jnp.dot(logit_grad.T, aux_out, preferred_element_type=jn...]
    pallas_call x0 -> x1, Pallas kernels: none -> 92.6 us  [local_step(): pl.pallas_call(kernel, name='step', out_shape=(jax.ShapeDtypeStruct((1, 6...]
    dot_general x13 -> x0, matrix products: 74.3 us -> none  [the longest x1 12 us: local(): jnp.dot(flat.T, hidden_grad, preferred_element_type=jnp.float32)]
    unnamed x8 -> x0, waiting for transfers between devices: 67.8 us -> none
    all_gather x2 -> x0, waiting for transfers between devices: 62.2 us -> none  [the longest x1 31.8 us: local(): all_rows = lax.all_gather(class_shard, 'dp', axis=0, tiled=True)]
    convert_element_type x4 -> x0, local copies, waits for them, and re-layouts: 35.6 us -> none  [the longest x2 18 us: local(): target.astype(jnp.float32)]
    all_gather x1 -> x0, local copies, waits for them, and re-layouts: 9.53 us -> none  [local(): lax.all_gather(patches, 'section', axis=2, tiled=True)]
    another operation x1 -> x4, local copies, waits for them, and re-layouts: 8.41 us -> 0.49 us  [pack(): extra = jnp.transpose(four[3].reshape(q, 3, 32), (1, 0, 2))]
  transfers between devices with their start and end apart: 7 -> 0, of which waited for: 7 -> 0; matrix products, arithmetic and copies ran while one was open for 27% -> 0% of each run, Pallas kernels for 0% -> 0%
where the time goes in v2:
time: 108 us
  Pallas kernels  92.6 us (86%)
  local copies, waits for them, and re-layouts  13.2 us (12%)
  other arithmetic  1.16 us (1%)
    pallas_call x1, Pallas kernels, local_step(): pl.pallas_call(kernel, name='step', out_shape=(jax.ShapeDtypeStruct((1, 6...  92.6 us
    unnamed x7, local copies, waits for them, and re-layouts  8.7 us
    slice x6, local copies, waits for them, and re-layouts, pack(): extra = jnp.transpose(four[3].reshape(q, 3, 32), (1, 0, 2))  2.48 us

profile of v2, /device:TPU:1, one launch (start us, length us, event | category | flops | bytes accessed | tf_op | source)
XLA Modules:
  0.0 107.7 jit_solution(1797818422510006106)
XLA Ops:
  0.6 0.0 copy-start
  0.6 1.2 %slice.63 = bf16[13,16,96]{0,2,1:T(8,128)(2,1)S(1)} slice(bf16[196,16,96]{0,2,1:T(8,128)(2,1)} %bitcast.18), slice={[183:196], [0:16], [0:96]} | slice | bytes 79872 | tf_op jit(solution)/shard_map/slice | solution.py:422
  1.9 0.2 copy.27
  2.1 0.1 reshape_squeeze.15
  2.3 0.0 copy-done
  2.3 0.2 slice.62
  2.5 0.2 copy.26
  2.7 0.4 fusion.1
  3.1 0.2 copy.18
  3.3 0.2 copy.24
  3.5 0.2 copy.21
  3.7 0.1 reshape_squeeze.13
  3.9 0.1 reshape_squeeze.14
  4.1 0.1 reshape_squeeze.12
  4.2 0.3 fusion
  4.5 0.2 copy.17
  4.8 0.2 copy.23
  5.0 0.2 copy.20
  5.3 1.2 %maximum_maximum_fusion.packed = bf16[2352,128]{1,0:T(8,128)(2,1)} fusion(bf16[624,32]{1,0:T(8,128)(2,1)S(1)} %bitcast.26, bf16[624,96]{1,0:T(8,128)(2,1)S(1)} %bitcast.27, bf16[576,32]{1,0:T(8,128)(2,1)S(1)} %bitcast.29, bf16[576,96]{1,0:T(8,128)(2,1)S(1)} %bitcast.32, bf16[576,32]{1,0:T(8,128)(2,1)S(1)} %bitcast.28, bf16[576,96]{1,0:T(8,128)(2,1)S(1)} %bitcast.33, ...), kind=kLoop, calls=%fused_computation | loop fusion | flops 4816896 | bytes 1204224 | tf_op jit(solution)/shard_map/concatenate | solution.py:424
  6.4 92.6 %step.1 = (f32[1,64,256]{2,1,0:T(8,128)}, f32[1,16,1024]{2,1,0:T(8,128)}, f32[1,64,768]{2,1,0:T(8,128)}, f32[1,64,512]{2,1,0:T(8,128)}, f32[1,704,512]{2,1,0:T(8,128)}) custom-call(bf16[3136,1024]{1,0:T(8,128)(2,1)} %bitcast.34, bf16[2352,128]{1,0:T(8,128)(2,1)} %maximum_maximum_fusion.packed, s32[16]{0:T(128)} %labels.1, bf16[1,1024,256]{2,1,0:T(8,128)(2,1)} %wf_h.1, ...), custom_call_target="tpu_custom_call" | custom-call | flops 24999999488 | bytes 16000000 | tf_op jit(solution)/shard_map/step/pallas_call | solution.py:441
  99.0 1.5 %copy.34 = f32[1,64,256]{2,1,0:T(8,128)} copy(f32[1,64,256]{2,1,0:T(8,128)} %get-tuple-element.16) | data formatting | bytes 131072
  100.5 1.5 %copy.35 = f32[1,16,1024]{2,1,0:T(8,128)} copy(f32[1,16,1024]{2,1,0:T(8,128)} %get-tuple-element.17) | data formatting | bytes 131072
  101.9 1.6 %copy.36 = f32[1,64,768]{2,1,0:T(8,128)} copy(f32[1,64,768]{2,1,0:T(8,128)} %get-tuple-element.18) | data formatting | bytes 393216
  103.6 1.6 %copy.37 = f32[1,64,512]{2,1,0:T(8,128)} copy(f32[1,64,512]{2,1,0:T(8,128)} %get-tuple-element.19) | data formatting | bytes 262144
  105.1 2.6 %copy.38 = f32[1,704,512]{2,1,0:T(8,128)} copy(f32[1,704,512]{2,1,0:T(8,128)} %get-tuple-element.20) | data formatting | bytes 2883584
  (4 shorter events, 0.1 us)
Async XLA Ops:
  0.6 1.6 %copy-start = (bf16[16,196,96]{1,2,0:T(8,128)(2,1)S(1)}, bf16[16,196,96]{1,2,0:T(8,128)(2,1)}, u32[]{:S(2)}) copy-start(bf16[16,196,96]{1,2,0:T(8,128)(2,1)} %param.9) | copy-start | bytes 1806340

commit v3 on v2

--- a/solution.py
+++ b/solution.py
@@ -25,7 +25,7 @@
 SIZES = (768, 768, 768, 832)
 CHUNKS = len(SIZES)
 PROWS = ROWS * SLICE // 128
-KINDS = (2, 1, 2, 1)
+KINDS = (2, 2, 1, 2)
 
 
 def dot(a, b):
@@ -53,9 +53,9 @@
 
 
 def kernel(
-    acts, packed, labels, wf_h, ws_h, wd_h, wa_h, wc_h,
+    acts, patches, labels, wf_h, ws_h, wd_h, wa_h, wc_h,
     gf, gs, gd, ga, gc,
-    x, feat, hid, pat, wf, ws, wd, wp, wa, wc, recon,
+    x, feat, hid, pat, raw, wf, ws, wd, wp, wa, wc, recon,
     pooled, poolb, auxall, poolall, stats, logits, backs, backr, agall, pgrad,
     target, acc_f, acc_s, acc_d, gaacc,
     pf, ps, pd, qf, qs, qd, tf, ts, td, rf, rs, rd,
@@ -76,7 +76,7 @@
     loads = [
         pltpu.make_async_copy(src, dst, local.at[i])
         for i, (src, dst) in enumerate(
-            [(packed, pat.at[me_s]), (wf_h.at[0], wf), (ws_h.at[0], ws)]
+            [(patches, raw), (wf_h.at[0], wf), (ws_h.at[0], ws)]
             + [
                 (acts.at[pl.ds(STARTS[c], SIZES[c]), :], x.at[pl.ds(STARTS[c], SIZES[c]), :])
                 for c in range(CHUNKS)
@@ -96,7 +96,6 @@
         return 0
 
     lax.fori_loop(1, DP, greet, 0)
-    pl.semaphore_wait(barrier, 3 + DP - 1)
 
     sent = [0] * CHUNKS
     started = []
@@ -116,12 +115,22 @@
             place, place, psend.at[chunk, 0], precv.at[chunk, half, source], {"section": up}
         ).wait_recv()
 
-    loads[0].wait()
-    for chunk in range(CHUNKS):
+    def own_y(chunk):
+        for half in range(2):
+            pass_on(chunk, me_s, half, up if half == 0 else down)
+            pass_on(chunk, me_s, half, down if half == 0 else up)
+
+    def own_x(chunk):
         for half in range(2):
             pass_on(chunk, me_s, half, across)
-            pass_on(chunk, me_s, half, up if half == 0 else down)
-            pass_on(chunk, me_s, half, down if half == 0 else up)
+
+    def pack(chunk):
+        q = SIZES[chunk] // 4
+        base = STARTS[chunk] * 3 // 4
+        fourth = raw[pl.ds(STARTS[chunk] + 3 * q, q), :]
+        for a in range(3):
+            pat[me_s, pl.ds(base + a * q, q), 0:SLICE] = raw[pl.ds(STARTS[chunk] + a * q, q), :]
+            pat[me_s, pl.ds(base + a * q, q), SLICE:128] = fourth[:, 32 * a:32 * (a + 1)]
 
     def stage1(chunk):
         for source, half, onward in (
@@ -179,94 +188,6 @@
 
     def rebuild(chunk):
         recon[rows_of(chunk), :] = dot(feat[rows_of(chunk), :], wp[...])
-
-    def spread(kind, src, dst):
-        def one(k, _):
-            peer = lax.rem(me_d + k, DP)
-            rcopy(src(peer), dst, dsend.at[kind, peer], drecv.at[kind, me_d], {"dp": peer}).start()
-            return 0
-
-        lax.fori_loop(1, DP, one, 0)
-
-    def collect(kind, slot):
-        def one(k, _):
-            peer = lax.rem(me_d + k, DP)
-            rcopy(slot(peer), slot(peer), dsend.at[kind, peer], drecv.at[kind, peer], {"dp": peer}).wait_recv()
-            return 0
-
-        lax.fori_loop(1, DP, one, 0)
-
-    loads[1].wait()
-    loads[2].wait()
-    forward(0)
-    forward(1)
-    stage1(0)
-    forward(2)
-    forward(3)
-
-    loads[7].wait()
-    pool_b = (pooled[...] * (1.0 / PIX)).astype(BF16)
-    aux_out = jnp.maximum(dot(pool_b, wa[...]), 0.0).astype(BF16)
-    auxall[me_d] = aux_out
-    spread(0, lambda peer: auxall.at[me_d], auxall.at[me_d])
-    for block in range(8):
-        poolb[block] = pool_b[:, 128 * block:128 * (block + 1)]
-    poolall[me_d] = poolb[chip]
-    spread(1, lambda peer: poolb.at[peer // 2], poolall.at[me_d])
-    stage1(1)
-
-    loads[8].wait()
-    source = lax.broadcasted_iota(jnp.int32, (PATCH, PATCH), 0)
-    place = lax.broadcasted_iota(jnp.int32, (PATCH, PATCH), 1)
-    tile, lane = place >> 7, place & 127
-    late = (tile >= 3).astype(jnp.int32)
-    origin = jnp.where(
-        lane < SLICE, SLICE * tile + lane, 6 * SLICE + SLICE * late + 32 * (tile - 3 * late) + lane - SLICE
-    )
-    wp[...] = dot(wd[...], (source == origin).astype(F32).astype(BF16)).astype(BF16)
-    rebuild(0)
-
-    loads[9].wait()
-    collect(0, lambda peer: auxall.at[peer])
-    every = auxall[...].reshape(DP * IMG, HEAD)
-    raw = dot_nt(wc[...], every)
-    logits[...] = raw
-    top = jnp.max(raw, axis=0, keepdims=True)
-    total = jnp.sum(jnp.exp(raw - top), axis=0, keepdims=True)
-    column = lax.broadcasted_iota(jnp.int32, (1, DP * IMG), 1)
-    line = jnp.zeros((1, DP * IMG), F32)
-    for image in range(IMG):
-        line = jnp.where(column == me_d * IMG + image, labels[image].astype(F32), line)
-    stats[me_d] = jnp.concatenate([top, total, line, jnp.zeros((5, DP * IMG), F32)], axis=0)
-    spread(2, lambda peer: stats.at[me_d], stats.at[me_d])
-    stage2(0)
-    stage1(2)
-    rebuild(1)
-
-    collect(2, lambda peer: stats.at[peer])
-    table = stats[...]
-    high = jnp.max(table[:, 0, :], axis=0, keepdims=True)
-    denominator = jnp.sum(table[:, 1, :] * jnp.exp(table[:, 0, :] - high), axis=0, keepdims=True)
-    label = jnp.sum(table[:, 2, :], axis=0, keepdims=True).astype(jnp.int32)
-    prob = jnp.exp(logits[...] - high) / denominator
-    number = lax.broadcasted_iota(jnp.int32, (CSHARD, DP * IMG), 0) + me_d * CSHARD
-    lg = ((prob - (number == label).astype(F32)) * 0.0625).astype(BF16)
-    backs[...] = dot_tn(lg, wc[...]).reshape(DP, IMG, HEAD)
-    spread(3, lambda peer: backs.at[peer], backr.at[me_d])
-    backr[me_d] = backs[me_d]
-    gc[0] = dot(lg, every)
-    stage2(1)
-    stage1(3)
-    rebuild(2)
-
-    collect(3, lambda peer: backr.at[peer])
-    aux_grad = jnp.where(auxall[me_d] > 0, jnp.sum(backr[...], axis=0), 0.0).astype(BF16)
-    agall[me_d] = aux_grad
-    spread(4, lambda peer: agall.at[me_d], agall.at[me_d])
-    pgrad[...] = dot_nt(aux_grad, wa[...]) * (1.0 / PIX)
-    stage2(2)
-    stage2(3)
-    rebuild(3)
 
     def assemble(chunk):
         q = SIZES[chunk] // 4
@@ -314,20 +235,118 @@
             acc_s[...] += part_s
             acc_f[...] += part_f
 
-    for chunk in range(CHUNKS - 1):
-        rg = decode_grad(chunk)
-        module_grads(chunk, *feature_grad(chunk, rg))
-
+    def spread(kind, src, dst):
+        def one(k, _):
+            peer = lax.rem(me_d + k, DP)
+            rcopy(src(peer), dst, dsend.at[kind, peer], drecv.at[kind, me_d], {"dp": peer}).start()
+            return 0
+
+        lax.fori_loop(1, DP, one, 0)
+
+    def collect(kind, slot):
+        def one(k, _):
+            peer = lax.rem(me_d + k, DP)
+            rcopy(slot(peer), slot(peer), dsend.at[kind, peer], drecv.at[kind, peer], {"dp": peer}).wait_recv()
+            return 0
+
+        lax.fori_loop(1, DP, one, 0)
+
+    loads[0].wait()
+    for chunk in range(CHUNKS):
+        pack(chunk)
+    loads[1].wait()
+    loads[2].wait()
+    forward(0)
+    pl.semaphore_wait(barrier, 3 + DP - 1)
+    own_x(0)
+    own_y(0)
+    own_y(1)
+    forward(1)
+    forward(2)
+    forward(3)
+
+    loads[7].wait()
+    pool_b = (pooled[...] * (1.0 / PIX)).astype(BF16)
+    aux_out = jnp.maximum(dot(pool_b, wa[...]), 0.0).astype(BF16)
+    auxall[me_d] = aux_out
+    spread(0, lambda peer: auxall.at[me_d], auxall.at[me_d])
+    for block in range(8):
+        poolb[block] = pool_b[:, 128 * block:128 * (block + 1)]
+    poolall[me_d] = poolb[chip]
+    own_x(1)
+
+    loads[8].wait()
+    source = lax.broadcasted_iota(jnp.int32, (PATCH, PATCH), 0)
+    place = lax.broadcasted_iota(jnp.int32, (PATCH, PATCH), 1)
+    tile, lane = place >> 7, place & 127
+    late = (tile >= 3).astype(jnp.int32)
+    origin = jnp.where(
+        lane < SLICE, SLICE * tile + lane, 6 * SLICE + SLICE * late + 32 * (tile - 3 * late) + lane - SLICE
+    )
+    wp[...] = dot(wd[...], (source == origin).astype(F32).astype(BF16)).astype(BF16)
+    stage1(0)
+    own_y(2)
+    rebuild(0)
+    rebuild(1)
+    rebuild(2)
+
+    loads[9].wait()
+    collect(0, lambda peer: auxall.at[peer])
+    every = auxall[...].reshape(DP * IMG, HEAD)
+    score = dot_nt(wc[...], every)
+    logits[...] = score
+    top = jnp.max(score, axis=0, keepdims=True)
+    total = jnp.sum(jnp.exp(score - top), axis=0, keepdims=True)
+    column = lax.broadcasted_iota(jnp.int32, (1, DP * IMG), 1)
+    line = jnp.zeros((1, DP * IMG), F32)
+    for image in range(IMG):
+        line = jnp.where(column == me_d * IMG + image, labels[image].astype(F32), line)
+    stats[me_d] = jnp.concatenate([top, total, line, jnp.zeros((5, DP * IMG), F32)], axis=0)
+    spread(2, lambda peer: stats.at[me_d], stats.at[me_d])
+    own_x(3)
+    rebuild(3)
+    stage1(1)
+
+    collect(2, lambda peer: stats.at[peer])
+    table = stats[...]
+    high = jnp.max(table[:, 0, :], axis=0, keepdims=True)
+    denominator = jnp.sum(table[:, 1, :] * jnp.exp(table[:, 0, :] - high), axis=0, keepdims=True)
+    label = jnp.sum(table[:, 2, :], axis=0, keepdims=True).astype(jnp.int32)
+    prob = jnp.exp(logits[...] - high) / denominator
+    number = lax.broadcasted_iota(jnp.int32, (CSHARD, DP * IMG), 0) + me_d * CSHARD
+    lg = ((prob - (number == label).astype(F32)) * 0.0625).astype(BF16)
+    backs[...] = dot_tn(lg, wc[...]).astype(BF16).reshape(DP, IMG, HEAD)
+    spread(3, lambda peer: backs.at[peer], backr.at[me_d])
+    backr[me_d] = backs[me_d]
+    gc[0] = dot(lg, every)
+    stage2(0)
+    own_x(2)
+    stage1(2)
+    rg = decode_grad(0)
+
+    collect(3, lambda peer: backr.at[peer])
+    aux_grad = jnp.where(auxall[me_d] > 0, jnp.sum(backr[...].astype(F32), axis=0), 0.0).astype(BF16)
+    agall[me_d] = aux_grad
+    spread(4, lambda peer: agall.at[me_d], agall.at[me_d])
+    spread(1, lambda peer: poolb.at[peer // 2], poolall.at[me_d])
+    pgrad[...] = dot_nt(aux_grad, wa[...]) * (1.0 / PIX)
+    stage2(1)
+    own_y(3)
+    module_grads(0, *feature_grad(0, rg))
+    stage2(2)
+    rg = decode_grad(1)
+    stage1(3)
+    module_grads(1, *feature_grad(1, rg))
     collect(1, lambda peer: poolall.at[peer])
     collect(4, lambda peer: agall.at[peer])
-    gaacc[...] = jnp.zeros_like(gaacc)
-
-    def aux_part(group, _):
-        gaacc[...] += dot_tn(poolall[group], agall[group]).astype(BF16).astype(F32)
-        return 0
-
-    lax.fori_loop(0, DP, aux_part, 0)
+    sums = jnp.zeros((128, HEAD), F32)
+    for group in range(DP):
+        sums += dot_tn(poolall[group], agall[group]).astype(BF16).astype(F32)
+    gaacc[...] = sums
     ga[0] = gaacc[pl.ds(pl.multiple_of(64 * core, 64), 64), :]
+    rg = decode_grad(2)
+    stage2(3)
+    module_grads(2, *feature_grad(2, rg))
 
     def pair(kind, mine, theirs):
         return rcopy(mine.at[1 - core], theirs, csend.at[kind], crecv.at[kind], {"dp": me_d + 1 - 2 * core})
@@ -413,15 +432,13 @@
     lax.fori_loop(1, 8, drain_chip, 0)
 
 
-def pack(patches):
-    rows = jnp.transpose(patches, (1, 0, 2)).reshape(ROWS, SLICE)
-    parts = []
-    for chunk in range(CHUNKS):
-        q = SIZES[chunk] // 4
-        four = lax.slice_in_dim(rows, STARTS[chunk], STARTS[chunk] + SIZES[chunk]).reshape(4, q, SLICE)
-        extra = jnp.transpose(four[3].reshape(q, 3, 32), (1, 0, 2))
-        parts.append(jnp.concatenate([four[:3], extra], axis=2).reshape(3 * q, 128))
-    return jnp.concatenate(parts, axis=0)
+def finish(*refs):
+    sems = refs[-1]
+    copies = [pltpu.make_async_copy(refs[i], refs[5 + i], sems.at[i]) for i in range(5)]
+    for copy in copies:
+        copy.start()
+    for copy in copies:
+        copy.wait()
 
 
 def local_step(acts, patches, labels, w_first, w_second, w_decode, w_aux, w_class):
@@ -429,23 +446,24 @@
     vmem = pl.BlockSpec(memory_space=pltpu.VMEM)
     big = max(SIZES)
     shapes = [
-        ((ROWS, C), BF16), ((ROWS, C), BF16), ((ROWS, BOT), BF16), ((SEC, PROWS, 128), BF16),
+        ((ROWS, C), BF16), ((ROWS, C), BF16), ((ROWS, BOT), BF16), ((SEC, PROWS, 128), BF16), ((ROWS, SLICE), BF16),
         ((C, BOT), BF16), ((BOT, C), BF16), ((C, PATCH), BF16), ((C, PATCH), BF16), ((C, HEAD), BF16),
         ((CSHARD, HEAD), BF16), ((ROWS, PATCH), F32),
         ((IMG, C), F32), ((8, IMG, 128), BF16), ((DP, IMG, HEAD), BF16), ((DP, IMG, 128), BF16),
-        ((DP, 8, DP * IMG), F32), ((CSHARD, DP * IMG), F32), ((DP, IMG, HEAD), F32), ((DP, IMG, HEAD), F32),
+        ((DP, 8, DP * IMG), F32), ((CSHARD, DP * IMG), F32), ((DP, IMG, HEAD), BF16), ((DP, IMG, HEAD), BF16),
         ((DP, IMG, HEAD), BF16), ((IMG, C), F32),
         ((big, PATCH), BF16), ((C, BOT), F32), ((BOT, C), F32), ((C, PATCH), F32), ((128, HEAD), F32),
         ((2, 8, 64, BOT), BF16), ((2, 8, 16, C), BF16), ((2, 8, 64, PATCH), BF16),
     ] + [((8, 64, BOT), BF16), ((8, 16, C), BF16), ((8, 64, PATCH), BF16)] * 3
-    return pl.pallas_call(
+    shapes_out = (
+        jax.ShapeDtypeStruct((1, 64, BOT), F32), jax.ShapeDtypeStruct((1, 16, C), F32),
+        jax.ShapeDtypeStruct((1, 64, PATCH), F32), jax.ShapeDtypeStruct((1, 64, HEAD), F32),
+        jax.ShapeDtypeStruct((1, CSHARD, HEAD), F32),
+    )
+    results = pl.pallas_call(
         kernel,
         name="step",
-        out_shape=(
-            jax.ShapeDtypeStruct((1, 64, BOT), F32), jax.ShapeDtypeStruct((1, 16, C), F32),
-            jax.ShapeDtypeStruct((1, 64, PATCH), F32), jax.ShapeDtypeStruct((1, 64, HEAD), F32),
-            jax.ShapeDtypeStruct((1, CSHARD, HEAD), F32),
-        ),
+        out_shape=shapes_out,
         in_specs=[any_spec, any_spec, pl.BlockSpec(memory_space=pltpu.SMEM)] + [any_spec] * 5,
         out_specs=[vmem] * 5,
         scratch_shapes=[pltpu.VMEM(shape, kind) for shape, kind in shapes] + [
@@ -460,9 +478,18 @@
         ),
         cost_estimate=pl.CostEstimate(flops=25 * 10**9, bytes_accessed=16 * 10**6, transcendentals=400000),
     )(
-        jnp.transpose(acts[0], (1, 0, 2)).reshape(ROWS, C), pack(patches), labels,
+        jnp.transpose(acts[0], (1, 0, 2)).reshape(ROWS, C),
+        jnp.transpose(patches, (1, 0, 2)).reshape(ROWS, SLICE), labels,
         w_first, w_second, w_decode, w_aux, w_class,
     )
+    return pl.pallas_call(
+        finish,
+        name="finish",
+        out_shape=shapes_out,
+        in_specs=[any_spec] * 5,
+        out_specs=[any_spec] * 5,
+        scratch_shapes=[pltpu.SemaphoreType.DMA((5,))],
+    )(*results)
 
 
 def solution(mesh):

time: 108 us -> 145 us (1.34)
  Pallas kernels: 92.6 us -> 141 us
  local copies, waits for them, and re-layouts: 13.2 us -> 2.3 us
    pallas_call x1 -> x2, Pallas kernels: 92.6 us -> 141 us  [the longest x1 82.7 us: local_step(): pl.pallas_call(kernel, name='step', out_shape=shapes_out, in_specs=[any_s...]
    unnamed x7 -> x0, local copies, waits for them, and re-layouts: 8.7 us -> none
    slice x12 -> x0, local copies, waits for them, and re-layouts: 3.95 us -> none  [the longest x6 2.48 us: pack(): extra = jnp.transpose(four[3].reshape(q, 3, 32), (1, 0, 2))]
    transpose x4 -> x1, local copies, waits for them, and re-layouts: 0.1 us -> 2.3 us  [local_step(): jnp.transpose(patches, (1, 0, 2)).reshape(ROWS, SLICE)]
where the time goes in v3:
time: 145 us
  Pallas kernels  141 us (97%)
  local copies, waits for them, and re-layouts  2.3 us (2%)
    pallas_call x1, Pallas kernels, local_step(): pl.pallas_call(kernel, name='step', out_shape=shapes_out, in_specs=[any_s...  82.7 us
    pallas_call x1, Pallas kernels, local_step(): pl.pallas_call(finish, name='finish', out_shape=shapes_out, in_specs=[any...  58.7 us

profile of v3, /device:TPU:1, one launch (start us, length us, event | category | flops | bytes accessed | tf_op | source)
XLA Modules:
  0.0 144.6 jit_solution(12102252318040269171)
XLA Ops:
  0.6 2.3 %copy.13 = bf16[196,16,96]{2,1,0:T(8,128)(2,1)} copy(bf16[196,16,96]{0,2,1:T(8,128)(2,1)} %bitcast.8) | data formatting | bytes 1204224 | tf_op jit(solution)/shard_map/transpose | solution.py:482
  2.9 82.7 %step.1 = (f32[1,64,256]{2,1,0:T(8,128)}, f32[1,16,1024]{2,1,0:T(8,128)}, f32[1,64,768]{2,1,0:T(8,128)}, f32[1,64,512]{2,1,0:T(8,128)}, f32[1,704,512]{2,1,0:T(8,128)}) custom-call(bf16[3136,1024]{1,0:T(8,128)(2,1)} %bitcast.9, bf16[3136,96]{1,0:T(8,128)(2,1)} %bitcast.7, s32[16]{0:T(128)} %labels.1, bf16[1,1024,256]{2,1,0:T(8,128)(2,1)} %wf_h.1, ...), custom_call_target="tpu_custom_call" | custom-call | flops 24999999488 | bytes 16000000 | tf_op jit(solution)/shard_map/step/pallas_call | solution.py:463
  85.7 58.7 %finish.1 = (f32[1,64,256]{2,1,0:T(8,128)}, f32[1,16,1024]{2,1,0:T(8,128)}, f32[1,64,768]{2,1,0:T(8,128)}, f32[1,64,512]{2,1,0:T(8,128)}, f32[1,704,512]{2,1,0:T(8,128)}) custom-call(f32[1,64,256]{2,1,0:T(8,128)} %get-tuple-element.10.refs_0_, f32[1,16,1024]{2,1,0:T(8,128)} %get-tuple-element.11.refs_1_, f32[1,64,768]{2,1,0:T(8,128)} %get-tuple-element.12.refs_2_, ...), custom_call_target="tpu_custom_call" | custom-call | tf_op jit(solution)/shard_map/finish/pallas_call | solution.py:485

commit v4 on v3

--- a/solution.py
+++ b/solution.py
@@ -433,12 +433,8 @@
 
 
 def finish(*refs):
-    sems = refs[-1]
-    copies = [pltpu.make_async_copy(refs[i], refs[5 + i], sems.at[i]) for i in range(5)]
-    for copy in copies:
-        copy.start()
-    for copy in copies:
-        copy.wait()
+    for source, out in zip(refs[:5], refs[5:]):
+        out[...] = source[...]
 
 
 def local_step(acts, patches, labels, w_first, w_second, w_decode, w_aux, w_class):
@@ -486,9 +482,8 @@
         finish,
         name="finish",
         out_shape=shapes_out,
-        in_specs=[any_spec] * 5,
-        out_specs=[any_spec] * 5,
-        scratch_shapes=[pltpu.SemaphoreType.DMA((5,))],
+        in_specs=[vmem] * 5,
+        out_specs=[vmem] * 5,
     )(*results)
 
 

time: 145 us -> 89.1 us (0.61)
  Pallas kernels: 141 us -> 85.6 us
    pallas_call x1, Pallas kernels: 58.7 us -> 2.87 us  [local_step(): pl.pallas_call(finish, name='finish', out_shape=shapes_out, in_specs=[vme...]
where the time goes in v4:
time: 89.1 us; the launch traced here: 88.5 us
  Pallas kernels  85.6 us (96%)
  local copies, waits for them, and re-layouts  2.3 us (3%)
    pallas_call x1, Pallas kernels, local_step(): pl.pallas_call(kernel, name='step', out_shape=shapes_out, in_specs=[any_s...  82.7 us
    pallas_call x1, Pallas kernels, local_step(): pl.pallas_call(finish, name='finish', out_shape=shapes_out, in_specs=[vme...  2.87 us
    transpose x1, local copies, waits for them, and re-layouts, local_step(): jnp.transpose(patches, (1, 0, 2)).reshape(ROWS, SLICE)  2.3 us

profile of v4, /device:TPU:1, one launch (start us, length us, event | category | flops | bytes accessed | tf_op | source)
XLA Modules:
  0.0 88.5 jit_solution(16696964461011796555)
XLA Ops:
  0.6 2.3 %copy.13 = bf16[196,16,96]{2,1,0:T(8,128)(2,1)} copy(bf16[196,16,96]{0,2,1:T(8,128)(2,1)} %bitcast.8) | data formatting | bytes 1204224 | tf_op jit(solution)/shard_map/transpose | solution.py:478
  2.9 82.7 %step.1 = (f32[1,64,256]{2,1,0:T(8,128)}, f32[1,16,1024]{2,1,0:T(8,128)}, f32[1,64,768]{2,1,0:T(8,128)}, f32[1,64,512]{2,1,0:T(8,128)}, f32[1,704,512]{2,1,0:T(8,128)}) custom-call(bf16[3136,1024]{1,0:T(8,128)(2,1)} %bitcast.9, bf16[3136,96]{1,0:T(8,128)(2,1)} %bitcast.7, s32[16]{0:T(128)} %labels.1, bf16[1,1024,256]{2,1,0:T(8,128)(2,1)} %wf_h.1, ...), custom_call_target="tpu_custom_call" | custom-call | flops 24999999488 | bytes 16000000 | tf_op jit(solution)/shard_map/step/pallas_call | solution.py:459
  85.7 2.9 %finish.1 = (f32[1,64,256]{2,1,0:T(8,128)}, f32[1,16,1024]{2,1,0:T(8,128)}, f32[1,64,768]{2,1,0:T(8,128)}, f32[1,64,512]{2,1,0:T(8,128)}, f32[1,704,512]{2,1,0:T(8,128)}) custom-call(f32[1,64,256]{2,1,0:T(8,128)} %get-tuple-element.10.refs_0_, f32[1,16,1024]{2,1,0:T(8,128)} %get-tuple-element.11.refs_1_, f32[1,64,768]{2,1,0:T(8,128)} %get-tuple-element.12.refs_2_, ...), custom_call_target="tpu_custom_call" | custom-call | tf_op jit(solution)/shard_map/finish/pallas_call | solution.py:481

commit v5 on v4

--- a/solution.py
+++ b/solution.py
@@ -54,7 +54,7 @@
 
 def kernel(
     acts, patches, labels, wf_h, ws_h, wd_h, wa_h, wc_h,
-    gf, gs, gd, ga, gc,
+    gf, gs, gd, ga, lgs, auxout,
     x, feat, hid, pat, raw, wf, ws, wd, wp, wa, wc, recon,
     pooled, poolb, auxall, poolall, stats, logits, backs, backr, agall, pgrad,
     target, acc_f, acc_s, acc_d, gaacc,
@@ -288,7 +288,6 @@
     own_y(2)
     rebuild(0)
     rebuild(1)
-    rebuild(2)
 
     loads[9].wait()
     collect(0, lambda peer: auxall.at[peer])
@@ -304,7 +303,9 @@
     stats[me_d] = jnp.concatenate([top, total, line, jnp.zeros((5, DP * IMG), F32)], axis=0)
     spread(2, lambda peer: stats.at[me_d], stats.at[me_d])
     own_x(3)
+    rebuild(2)
     rebuild(3)
+    stage2(0)
     stage1(1)
 
     collect(2, lambda peer: stats.at[peer])
@@ -318,25 +319,75 @@
     backs[...] = dot_tn(lg, wc[...]).astype(BF16).reshape(DP, IMG, HEAD)
     spread(3, lambda peer: backs.at[peer], backr.at[me_d])
     backr[me_d] = backs[me_d]
-    gc[0] = dot(lg, every)
-    stage2(0)
+    lgs[...] = lg
+    auxout[...] = every
     own_x(2)
     stage1(2)
+    own_y(3)
     rg = decode_grad(0)
 
     collect(3, lambda peer: backr.at[peer])
     aux_grad = jnp.where(auxall[me_d] > 0, jnp.sum(backr[...].astype(F32), axis=0), 0.0).astype(BF16)
     agall[me_d] = aux_grad
+    pgrad[...] = dot_nt(aux_grad, wa[...]) * (1.0 / PIX)
+    module_grads(0, *feature_grad(0, rg))
+    stage2(1)
+    stage2(2)
     spread(4, lambda peer: agall.at[me_d], agall.at[me_d])
     spread(1, lambda peer: poolb.at[peer // 2], poolall.at[me_d])
-    pgrad[...] = dot_nt(aux_grad, wa[...]) * (1.0 / PIX)
-    stage2(1)
-    own_y(3)
-    module_grads(0, *feature_grad(0, rg))
-    stage2(2)
+    stage1(3)
     rg = decode_grad(1)
-    stage1(3)
     module_grads(1, *feature_grad(1, rg))
+    stage2(3)
+    rg_before = decode_grad(2)
+
+    def pair(kind, mine, theirs):
+        return rcopy(mine.at[1 - core], theirs, csend.at[kind], crecv.at[kind], {"dp": me_d + 1 - 2 * core})
+
+    def split(acc, out, rows):
+        whole = acc[...].astype(BF16).reshape(8, 2, rows, acc.shape[1])
+        out[0] = whole[:, 0]
+        out[1] = whole[:, 1]
+
+    def chip_sum(kind, mine, theirs, out, got):
+        pair(kind, mine, theirs).wait_recv()
+        out[...] = (mine[core].astype(F32) + theirs[...].astype(F32)).astype(BF16)
+
+        def one(k, _):
+            peer = lax.rem(chip + k, 8)
+            rcopy(
+                out.at[peer], got.at[chip], tsend.at[kind, peer], trecv.at[kind, chip], {"dp": 2 * peer + core}
+            ).start()
+            return 0
+
+        lax.fori_loop(1, 8, one, 0)
+        got[chip] = out[chip]
+
+    def total_sum(kind, got):
+        def one(k, _):
+            peer = lax.rem(chip + k, 8)
+            rcopy(
+                got.at[peer], got.at[peer], tsend.at[kind, peer], trecv.at[kind, peer], {"dp": 2 * peer + core}
+            ).wait_recv()
+            return 0
+
+        lax.fori_loop(1, 8, one, 0)
+        return jnp.sum(got[...].astype(F32), axis=0)
+
+    last = CHUNKS - 1
+    rg = decode_grad(last)
+    split(acc_d, pd, 64)
+    pair(0, pd, qd).start()
+    module_grads(last - 1, *feature_grad(last - 1, rg_before))
+    chip_sum(0, pd, qd, td, rd)
+    module_grads(last, *feature_grad(last, rg))
+    split(acc_f, pf, 64)
+    pair(1, pf, qf).start()
+    split(acc_s, ps, 16)
+    pair(2, ps, qs).start()
+    chip_sum(1, pf, qf, tf, rf)
+    chip_sum(2, ps, qs, ts, rs)
+
     collect(1, lambda peer: poolall.at[peer])
     collect(4, lambda peer: agall.at[peer])
     sums = jnp.zeros((128, HEAD), F32)
@@ -344,57 +395,6 @@
         sums += dot_tn(poolall[group], agall[group]).astype(BF16).astype(F32)
     gaacc[...] = sums
     ga[0] = gaacc[pl.ds(pl.multiple_of(64 * core, 64), 64), :]
-    rg = decode_grad(2)
-    stage2(3)
-    module_grads(2, *feature_grad(2, rg))
-
-    def pair(kind, mine, theirs):
-        return rcopy(mine.at[1 - core], theirs, csend.at[kind], crecv.at[kind], {"dp": me_d + 1 - 2 * core})
-
-    def split(acc, out, rows):
-        whole = acc[...].astype(BF16).reshape(8, 2, rows, acc.shape[1])
-        out[0] = whole[:, 0]
-        out[1] = whole[:, 1]
-
-    def chip_sum(kind, mine, theirs, out, got):
-        pair(kind, mine, theirs).wait_recv()
-        out[...] = (mine[core].astype(F32) + theirs[...].astype(F32)).astype(BF16)
-
-        def one(k, _):
-            peer = lax.rem(chip + k, 8)
-            rcopy(
-                out.at[peer], got.at[chip], tsend.at[kind, peer], trecv.at[kind, chip], {"dp": 2 * peer + core}
-            ).start()
-            return 0
-
-        lax.fori_loop(1, 8, one, 0)
-        got[chip] = out[chip]
-
-    def total_sum(kind, got):
-        def one(k, _):
-            peer = lax.rem(chip + k, 8)
-            rcopy(
-                got.at[peer], got.at[peer], tsend.at[kind, peer], trecv.at[kind, peer], {"dp": 2 * peer + core}
-            ).wait_recv()
-            return 0
-
-        lax.fori_loop(1, 8, one, 0)
-        return jnp.sum(got[...].astype(F32), axis=0)
-
-    last = CHUNKS - 1
-    rg = decode_grad(last)
-    split(acc_d, pd, 64)
-    pair(0, pd, qd).start()
-    fg, hg = feature_grad(last, rg)
-    chip_sum(0, pd, qd, td, rd)
-    module_grads(last, fg, hg)
-    split(acc_f, pf, 64)
-    pair(1, pf, qf).start()
-    split(acc_s, ps, 16)
-    pair(2, ps, qs).start()
-    chip_sum(1, pf, qf, tf, rf)
-    chip_sum(2, ps, qs, ts, rs)
-
     gsum = total_sum(0, rd)
     for s in range(SEC):
         if s < 6:
@@ -432,9 +432,10 @@
     lax.fori_loop(1, 8, drain_chip, 0)
 
 
-def finish(*refs):
-    for source, out in zip(refs[:5], refs[5:]):
+def finish(gf, gs, gd, ga, lgs, auxout, of, os, od, oa, oc):
+    for source, out in ((gf, of), (gs, os), (gd, od), (ga, oa)):
         out[...] = source[...]
+    oc[0] = dot(lgs[...], auxout[...])
 
 
 def local_step(acts, patches, labels, w_first, w_second, w_decode, w_aux, w_class):
@@ -459,9 +460,11 @@
     results = pl.pallas_call(
         kernel,
         name="step",
-        out_shape=shapes_out,
+        out_shape=shapes_out[:4] + (
+            jax.ShapeDtypeStruct((CSHARD, DP * IMG), BF16), jax.ShapeDtypeStruct((DP * IMG, HEAD), BF16),
+        ),
         in_specs=[any_spec, any_spec, pl.BlockSpec(memory_space=pltpu.SMEM)] + [any_spec] * 5,
-        out_specs=[vmem] * 5,
+        out_specs=[vmem] * 6,
         scratch_shapes=[pltpu.VMEM(shape, kind) for shape, kind in shapes] + [
             pltpu.SemaphoreType.DMA((10,)),
             pltpu.SemaphoreType.DMA((CHUNKS, 14)), pltpu.SemaphoreType.DMA((CHUNKS, 2, SEC)),
@@ -482,7 +485,7 @@
         finish,
         name="finish",
         out_shape=shapes_out,
-        in_specs=[vmem] * 5,
+        in_specs=[vmem] * 6,
         out_specs=[vmem] * 5,
     )(*results)
 

time: 89.1 us -> 82.3 us (0.924)
  Pallas kernels: 85.6 us -> 78.1 us
    pallas_call x1, Pallas kernels: 82.7 us -> 75.3 us  [local_step(): pl.pallas_call(kernel, name='step', out_shape=shapes_out[:4] + (jax.Shape...]
where the time goes in v5:
time: 82.3 us; the launch traced here: 81 us
  Pallas kernels  78.1 us (95%)
  local copies, waits for them, and re-layouts  2.3 us (3%)
    pallas_call x1, Pallas kernels, local_step(): pl.pallas_call(kernel, name='step', out_shape=shapes_out[:4] + (jax.Shape...  75.3 us
    pallas_call x1, Pallas kernels, local_step(): pl.pallas_call(finish, name='finish', out_shape=shapes_out, in_specs=[vme...  2.8 us
    transpose x1, local copies, waits for them, and re-layouts, local_step(): jnp.transpose(patches, (1, 0, 2)).reshape(ROWS, SLICE)  2.3 us

profile of v5, /device:TPU:1, one launch (start us, length us, event | category | flops | bytes accessed | tf_op | source)
XLA Modules:
  0.0 81.0 jit_solution(3860057001172128566)
XLA Ops:
  0.6 2.3 %copy.13 = bf16[196,16,96]{2,1,0:T(8,128)(2,1)} copy(bf16[196,16,96]{0,2,1:T(8,128)(2,1)} %bitcast.8) | data formatting | bytes 1204224 | tf_op jit(solution)/shard_map/transpose | solution.py:481
  2.9 75.3 %step.1 = (f32[1,64,256]{2,1,0:T(8,128)}, f32[1,16,1024]{2,1,0:T(8,128)}, f32[1,64,768]{2,1,0:T(8,128)}, f32[1,64,512]{2,1,0:T(8,128)}, bf16[704,256]{1,0:T(8,128)(2,1)}, /*index=5*/bf16[256,512]{1,0:T(8,128)(2,1)}) custom-call(bf16[3136,1024]{1,0:T(8,128)(2,1)} %bitcast.9, bf16[3136,96]{1,0:T(8,128)(2,1)} %bitcast.7, s32[16]{0:T(128)} %labels.1, ...), custom_call_target="tpu_custom_call" | custom-call | flops 24999999488 | bytes 16000000 | tf_op jit(solution)/shard_map/step/pallas_call | solution.py:460
  78.2 2.8 %finish.1 = (f32[1,64,256]{2,1,0:T(8,128)}, f32[1,16,1024]{2,1,0:T(8,128)}, f32[1,64,768]{2,1,0:T(8,128)}, f32[1,64,512]{2,1,0:T(8,128)}, f32[1,704,512]{2,1,0:T(8,128)}) custom-call(f32[1,64,256]{2,1,0:T(8,128)} %get-tuple-element.11.gf, f32[1,16,1024]{2,1,0:T(8,128)} %get-tuple-element.12.gs, f32[1,64,768]{2,1,0:T(8,128)} %get-tuple-element.13.gd, ...), custom_call_target="tpu_custom_call" | custom-call | tf_op jit(solution)/shard_map/finish/pallas_call | solution.py:484

commit v6 on v5

--- a/solution.py
+++ b/solution.py
@@ -132,7 +132,14 @@
             pat[me_s, pl.ds(base + a * q, q), 0:SLICE] = raw[pl.ds(STARTS[chunk] + a * q, q), :]
             pat[me_s, pl.ds(base + a * q, q), SLICE:128] = fourth[:, 32 * a:32 * (a + 1)]
 
-    def stage1(chunk):
+    def stage1_across(chunk):
+        for half in range(2):
+            arrive(chunk, across, half)
+            pass_on(chunk, across, half, up if half == 0 else down)
+        for half in range(2):
+            pass_on(chunk, across, half, down if half == 0 else up)
+
+    def stage1_along(chunk):
         for source, half, onward in (
             (at(side, 3), 0, up), (at(side, 1), 1, down), (at(side, 3), 1, None), (at(side, 1), 0, None)
         ):
@@ -141,11 +148,11 @@
                 pass_on(chunk, source, half, onward)
             if KINDS[chunk] == 1:
                 pass_on(chunk, source, half, across)
+
+    def stage1(chunk):
         if KINDS[chunk] == 2:
-            for half in range(2):
-                arrive(chunk, across, half)
-                pass_on(chunk, across, half, up if half == 0 else down)
-                pass_on(chunk, across, half, down if half == 0 else up)
+            stage1_across(chunk)
+        stage1_along(chunk)
 
     def stage2(chunk):
         if KINDS[chunk] == 1:
@@ -330,14 +337,15 @@
     aux_grad = jnp.where(auxall[me_d] > 0, jnp.sum(backr[...].astype(F32), axis=0), 0.0).astype(BF16)
     agall[me_d] = aux_grad
     pgrad[...] = dot_nt(aux_grad, wa[...]) * (1.0 / PIX)
-    module_grads(0, *feature_grad(0, rg))
+    fg, hg = feature_grad(0, rg)
     stage2(1)
+    stage1_across(3)
+    module_grads(0, fg, hg)
     stage2(2)
     spread(4, lambda peer: agall.at[me_d], agall.at[me_d])
     spread(1, lambda peer: poolb.at[peer // 2], poolall.at[me_d])
-    stage1(3)
-    rg = decode_grad(1)
-    module_grads(1, *feature_grad(1, rg))
+    stage1_along(3)
+    rg_first = decode_grad(1)
     stage2(3)
     rg_before = decode_grad(2)
 
@@ -378,8 +386,9 @@
     rg = decode_grad(last)
     split(acc_d, pd, 64)
     pair(0, pd, qd).start()
-    module_grads(last - 1, *feature_grad(last - 1, rg_before))
+    module_grads(1, *feature_grad(1, rg_first))
     chip_sum(0, pd, qd, td, rd)
+    module_grads(2, *feature_grad(2, rg_before))
     module_grads(last, *feature_grad(last, rg))
     split(acc_f, pf, 64)
     pair(1, pf, qf).start()

time: 82.3 us -> 81.2 us (0.987); the launches traced: 81 us -> 81.1 us
  no operation moved by 1% of the time
where the time goes in v6:
time: 81.2 us; the launch traced here: 81.1 us
  Pallas kernels  78.1 us (96%)
  local copies, waits for them, and re-layouts  2.3 us (3%)
    pallas_call x1, Pallas kernels, local_step(): pl.pallas_call(kernel, name='step', out_shape=shapes_out[:4] + (jax.Shape...  75.3 us
    pallas_call x1, Pallas kernels, local_step(): pl.pallas_call(finish, name='finish', out_shape=shapes_out, in_specs=[vme...  2.8 us
    transpose x1, local copies, waits for them, and re-layouts, local_step(): jnp.transpose(patches, (1, 0, 2)).reshape(ROWS, SLICE)  2.3 us

profile of v6, /device:TPU:1, one launch (start us, length us, event | category | flops | bytes accessed | tf_op | source)
XLA Modules:
  0.0 81.1 jit_solution(8016470360450057526)
XLA Ops:
  0.6 2.3 %copy.13 = bf16[196,16,96]{2,1,0:T(8,128)(2,1)} copy(bf16[196,16,96]{0,2,1:T(8,128)(2,1)} %bitcast.8) | data formatting | bytes 1204224 | tf_op jit(solution)/shard_map/transpose | solution.py:490
  2.9 75.3 %step.1 = (f32[1,64,256]{2,1,0:T(8,128)}, f32[1,16,1024]{2,1,0:T(8,128)}, f32[1,64,768]{2,1,0:T(8,128)}, f32[1,64,512]{2,1,0:T(8,128)}, bf16[704,256]{1,0:T(8,128)(2,1)}, /*index=5*/bf16[256,512]{1,0:T(8,128)(2,1)}) custom-call(bf16[3136,1024]{1,0:T(8,128)(2,1)} %bitcast.9, bf16[3136,96]{1,0:T(8,128)(2,1)} %bitcast.7, s32[16]{0:T(128)} %labels.1, ...), custom_call_target="tpu_custom_call" | custom-call | flops 24999999488 | bytes 16000000 | tf_op jit(solution)/shard_map/step/pallas_call | solution.py:469
  78.2 2.8 %finish.1 = (f32[1,64,256]{2,1,0:T(8,128)}, f32[1,16,1024]{2,1,0:T(8,128)}, f32[1,64,768]{2,1,0:T(8,128)}, f32[1,64,512]{2,1,0:T(8,128)}, f32[1,704,512]{2,1,0:T(8,128)}) custom-call(f32[1,64,256]{2,1,0:T(8,128)} %get-tuple-element.11.gf, f32[1,16,1024]{2,1,0:T(8,128)} %get-tuple-element.12.gs, f32[1,64,768]{2,1,0:T(8,128)} %get-tuple-element.13.gd, ...), custom_call_target="tpu_custom_call" | custom-call | tf_op jit(solution)/shard_map/finish/pallas_call | solution.py:493
